TPU v7x, 128 devices: a whole 4x4x4 slice. The times are simulated.
128 devices in a mesh: replica: 32 (over y, x, z_hi), tensor: 4 (over z_lo, core).
Axes of the slice: x: 4, y: 4, z: 4 (z_hi: 2, z_lo: 2; z = z_hi * 2 + z_lo), core: 2. Of those that a mesh axis runs over, the one named last changes fastest.
Arguments:
- weights: bfloat16 [32, 7168, 2048], P('replica', 'tensor'), may hold values from -6 to 6
- hidden: bfloat16 [32, 2, 512, 7168], P('replica', None, None, 'tensor'), may hold values from -6 to 6
- targets: bfloat16 [32, 2, 512, 2048], P('replica'), may hold values from -6 to 6
- norm_gain: float32 [2048], replicated, may hold values from 0.5 to 2
- stragglers: int32 [2, 32], replicated, may hold values 0 or 1
Outputs:
- new_weights: bfloat16 [32, 7168, 2048], P('replica', 'tensor')
All inputs are finite; a program needn't handle non-finite values.
Results may differ from a plain program's by a relative error of at most 0.011.
Values may be sent and summed in bfloat16 or wider, within the bound.
No kernel may reach another device: no remote copies, remote signals or barrier semaphores. Data moves between devices by JAX's collectives and lax.ppermute only.
A program may use at most 128 MiB of HBM per device.

v0:
```python
import jax
import jax.numpy as jnp
from jax import lax
from jax.sharding import PartitionSpec as P

FF = 7168
STEPS = 2


eps = 1e-05
learn_rate = 0.5


def partner(block, axis, apart):
    count = lax.axis_size(axis)
    route = []
    for low in range(count):
        high = low | 1 << apart
        if high != low and high < count:
            route += [(low, high), (high, low)]
    return lax.ppermute(block, axis, route)


def contract_rows(left, right):
    return lax.dot_general(
        left, right, (((0,), (0,)), ((), ())), preferred_element_type=jnp.float32
    )


def norm_backward(outputs, target_rows, norm_gain):
    squares = jnp.mean(outputs * outputs, axis=-1, keepdims=True)
    inverse = lax.rsqrt(squares + eps)
    normed = outputs * inverse
    weighted = (normed * norm_gain - target_rows.astype(jnp.float32)) * norm_gain
    cross_mean = jnp.mean(weighted * normed, axis=-1, keepdims=True)
    return (inverse * (weighted - normed * cross_mean)).astype(jnp.bfloat16)


def on_device(weights, hidden, targets, norm_gain, stragglers):
    replica_index = lax.axis_index("replica")
    levels = lax.axis_size("replica").bit_length() - 1
    factor = FF ** (-0.5)
    weight_block = weights[0]
    for update_step in range(STEPS):
        bit_index = update_step % levels
        hidden_rows = hidden[0, update_step]
        target_rows = targets[0, update_step]
        terms = factor * jnp.dot(hidden_rows, weight_block, preferred_element_type=jnp.float32)
        outputs = lax.psum(terms.astype(jnp.bfloat16), "tensor").astype(jnp.float32)
        grad_out = norm_backward(outputs, target_rows, norm_gain)
        grad_weight = (factor * contract_rows(hidden_rows, grad_out)).astype(jnp.bfloat16)
        updated = (
            weight_block.astype(jnp.float32) - learn_rate * grad_weight.astype(jnp.float32)
        ).astype(jnp.bfloat16)
        paired = partner(updated, "replica", bit_index)
        partner_index = jnp.bitwise_xor(replica_index, jnp.int32(1 << bit_index))
        mask_row = stragglers[update_step]
        self_late = lax.dynamic_index_in_dim(mask_row, replica_index, keepdims=False)
        partner_late = lax.dynamic_index_in_dim(mask_row, partner_index, keepdims=False)
        keep_pair = (self_late == 0) & (partner_late == 0)
        averaged = ((updated.astype(jnp.float32) + paired.astype(jnp.float32)) * 0.5).astype(
            jnp.bfloat16
        )
        weight_block = jnp.where(keep_pair, averaged, updated)
    return weight_block[None]


def solution(mesh):
    placed = (
        P("replica", "tensor", None),
        P("replica", None, None, "tensor"),
        P("replica", None, None, None),
        P(),
        P(),
    )
    return jax.shard_map(
        on_device,
        mesh=mesh,
        in_specs=placed,
        out_specs=P("replica", "tensor", None),
        check_vma=False,
    )
```

profile of v0, /device:TPU:1, one launch (start us, length us, event | category | flops | bytes accessed | tf_op | source)
XLA Modules:
  0.0 542.5 jit_solution(9329195445584160518)
XLA Ops:
  6.5 8.9 %multiply_convert_fusion.5 = bf16[512,2048]{1,0:T(8,128)(2,1)} fusion(bf16[1,1792,2048]{2,1,0:T(8,128)(2,1)} %param.5, bf16[1,2,512,1792]{3,2,1,0:T(8,128)(2,1)} %param.6), kind=kOutput, calls=%fused_computation.38 | convolution fusion | flops 3760193536 | bytes 11272192 | tf_op jit(solution)/shard_map/dot_general | solution.py:48
  15.5 0.0 all-reduce.3.cloned.1.call-update
  15.5 0.0 copy-start.6
  15.5 0.0 all-reduce.5.cloned.1.call-start
  15.6 9.9 %copy.6 = bf16[1,1792,2048]{1,2,0:T(8,128)(2,1)} copy(bf16[1,1792,2048]{2,1,0:T(8,128)(2,1)} %param.5) | data formatting | bytes 14680064 | tf_op args[0]
  25.5 51.2 %all-reduce.3.cloned.1.call-done = bf16[512,2048]{1,0:T(8,128)(2,1)} async-done(((bf16[512,2048]{1,0:T(8,128)(2,1)}), bf16[512,2048]{1,0:T(8,128)(2,1)}) %all-reduce.3.cloned.1.call-update) | async-done | bytes 2097168 | tf_op jit(solution)/shard_map/psum | solution.py:49
  76.7 2.2 fusion.19
  79.0 3.7 fusion.15
  82.7 9.9 %fusion.1 = bf16[1792,2048]{0,1:T(8,128)(2,1)} fusion(bf16[1,1792,2048]{1,2,0:T(8,128)(2,1)} %copy.6, bf16[512,2048]{1,0:T(8,128)(2,1)S(1)} %copy-done, f32[512]{0:T(512)S(1)} %broadcast_multiply_fusion.1, f32[2048]{0:T(1024)S(1)} %copy-done.6, f32[512]{0:T(512)S(1)} %add_rsqrt_fusion.1, bf16[1,2,512,2048]{3,2,1,0:T(8,128)(2,1)S(1)} %copy-done.4, ...), kind=kOutput, calls=%fused_computation.3 | convolution fusion | flops 3794272256 | bytes 20721664 | tf_op jit(solution)/shard_map/dot_general | solution.py:25
  92.6 2.6 collective-permute-start
  95.2 0.7 constant_dynamic-slice_fusion
  97.1 156.6 %collective-permute-done = bf16[1792,2048]{0,1:T(8,128)(2,1)} collective-permute-done((bf16[1792,2048]{0,1:T(8,128)(2,1)}, bf16[1792,2048]{0,1:T(8,128)(2,1)}, u32[]{:S(2)}, u32[]{:S(2)}) %collective-permute-start) | collective-permute-done | bytes 7340064 | tf_op jit(solution)/shard_map/ppermute | solution.py:21
  253.7 13.1 %fusion.29 = bf16[512,2048]{1,0:T(8,128)(2,1)} fusion(bf16[1,2,512,1792]{3,2,1,0:T(8,128)(2,1)} %param.6, bf16[1792,2048]{0,1:T(8,128)(2,1)} %fusion.1, bf16[1792,2048]{0,1:T(8,128)(2,1)} %collective-permute-done, pred[]{:T(512)} %bitcast.1), kind=kOutput, calls=%fused_computation.39 | convolution fusion | flops 3782213632 | bytes 18612736 | tf_op jit(solution)/shard_map/dot_general | solution.py:48
  266.8 0.0 all-reduce.5.cloned.1.call-update
  266.8 59.5 %all-reduce.5.cloned.1.call-done = bf16[512,2048]{1,0:T(8,128)(2,1)} async-done(((bf16[512,2048]{1,0:T(8,128)(2,1)}), bf16[512,2048]{1,0:T(8,128)(2,1)}) %all-reduce.5.cloned.1.call-update) | async-done | bytes 2097168 | tf_op jit(solution)/shard_map/psum | solution.py:49
  326.3 2.2 fusion.26
  328.6 3.7 fusion.22
  332.3 14.4 %fusion = bf16[1792,2048]{0,1:T(8,128)(2,1)S(1)} fusion(bf16[512,2048]{1,0:T(8,128)(2,1)S(1)} %copy-done.1, f32[512]{0:T(512)S(1)} %broadcast_multiply_fusion, f32[512]{0:T(512)S(1)} %add_rsqrt_fusion, f32[2048]{0:T(1024)S(1)} %copy-done.6, bf16[1,2,512,2048]{3,2,1,0:T(8,128)(2,1)S(1)} %copy-done.5, bf16[1,2,512,1792]{3,2,1,0:T(8,128)(2,1)} %param.6, ...), kind=kOutput, calls=%fused_computation.1 | convolution fusion | flops 3816292352 | bytes 28062208 | tf_op jit(solution)/shard_map/dot_general | solution.py:25
  346.7 3.0 copy-done.2
  349.7 1.2 collective-permute-start.1
  352.2 156.7 %collective-permute-done.1 = bf16[1792,2048]{0,1:T(8,128)(2,1)S(1)} collective-permute-done((bf16[1792,2048]{0,1:T(8,128)(2,1)S(1)}, bf16[1792,2048]{0,1:T(8,128)(2,1)S(1)}, u32[]{:S(2)}, u32[]{:S(2)}) %collective-permute-start.1) | collective-permute-done | bytes 7340064 | tf_op jit(solution)/shard_map/ppermute | solution.py:21
  509.0 3.0 copy-done.3
  511.9 13.3 %fusion.4 = bf16[1,1792,2048]{1,2,0:T(8,128)(2,1)} fusion(bf16[1792,2048]{0,1:T(8,128)(2,1)} %copy-done.2, bf16[1792,2048]{0,1:T(8,128)(2,1)} %copy-done.3, pred[]{:T(512)} %bitcast), kind=kLoop, calls=%fused_computation.10 | loop fusion | flops 22020096 | bytes 22020096 | tf_op jit(solution)/shard_map/broadcast_in_dim | solution.py:65
  525.3 10.4 %copy.8 = bf16[1,1792,2048]{2,1,0:T(8,128)(2,1)} copy(bf16[1,1792,2048]{1,2,0:T(8,128)(2,1)} %fusion.4) | data formatting | bytes 14680064 | tf_op jit(solution)/shard_map/broadcast_in_dim | solution.py:65
  (19 shorter events, 0.1 us)
Async XLA Ops:
  6.5 70.2 %all-reduce.3.cloned.1.call-start = ((), (), s32[]{:S(2)}) async-start(), calls=%async_computation | async-start | bytes 4194304 | tf_op jit(solution)/shard_map/psum | solution.py:49
  15.5 63.5 %copy-start.6 = (f32[2048]{0:T(1024)S(1)}, f32[2048]{0:T(1024)}, u32[]{:S(2)}) copy-start(f32[2048]{0:T(1024)} %param.8) | copy-start | bytes 24580
  15.5 310.8 %all-reduce.5.cloned.1.call-start = ((), (), s32[]{:S(2)}) async-start(), calls=%async_computation.1 | async-start | bytes 4194304 | tf_op jit(solution)/shard_map/psum | solution.py:49
  76.7 5.9 %copy-start = (bf16[512,2048]{1,0:T(8,128)(2,1)S(1)}, bf16[512,2048]{1,0:T(8,128)(2,1)}, u32[]{:S(2)}) copy-start(bf16[512,2048]{1,0:T(8,128)(2,1)} %all-reduce.3.cloned.1.call-done) | copy-start | bytes 6291460
  76.7 5.9 %copy-start.4 = (bf16[1,2,512,2048]{3,2,1,0:T(8,128)(2,1)S(1)}, bf16[1,2,512,2048]{3,2,1,0:T(8,128)(2,1)}, u32[]{:S(2)}) copy-start(bf16[1,2,512,2048]{3,2,1,0:T(8,128)(2,1)} %param.7) | copy-start | bytes 12582916
  82.7 12.5 %copy-start.7 = (s32[2,32]{1,0:T(2,128)S(1)}, s32[2,32]{1,0:T(2,128)}, u32[]{:S(2)}) copy-start(s32[2,32]{1,0:T(2,128)} %param.9) | copy-start | bytes 772
  92.6 161.1 %collective-permute-start = (bf16[1792,2048]{0,1:T(8,128)(2,1)}, bf16[1792,2048]{0,1:T(8,128)(2,1)}, u32[]{:S(2)}, u32[]{:S(2)}) collective-permute-start(bf16[1792,2048]{0,1:T(8,128)(2,1)} %fusion.1), channel_id=1, source_target_pairs={{0,4},{4,0},{8,12},{12,8},{16,20},{20,16},{24,28},{28,24},{32,36},... | collective-permute-start | bytes 22020104 | tf_op jit(solution)/shard_map/ppermute | solution.py:21
  326.3 5.9 %copy-start.1 = (bf16[512,2048]{1,0:T(8,128)(2,1)S(1)}, bf16[512,2048]{1,0:T(8,128)(2,1)}, u32[]{:S(2)}) copy-start(bf16[512,2048]{1,0:T(8,128)(2,1)} %all-reduce.5.cloned.1.call-done) | copy-start | bytes 6291460
  326.3 5.9 %copy-start.5 = (bf16[1,2,512,2048]{3,2,1,0:T(8,128)(2,1)S(1)}, bf16[1,2,512,2048]{3,2,1,0:T(8,128)(2,1)}, u32[]{:S(2)}) copy-start(bf16[1,2,512,2048]{3,2,1,0:T(8,128)(2,1)} %param.7) | copy-start | bytes 12582916
  346.7 3.1 copy-start.2
  349.7 159.2 %collective-permute-start.1 = (bf16[1792,2048]{0,1:T(8,128)(2,1)S(1)}, bf16[1792,2048]{0,1:T(8,128)(2,1)S(1)}, u32[]{:S(2)}, u32[]{:S(2)}) collective-permute-start(bf16[1792,2048]{0,1:T(8,128)(2,1)S(1)} %fusion), channel_id=1, source_target_pairs={{0,8},{8,0},{4,12},{12,4},{16,24},{24,16},{20,28},{28,20},{32,40},... | collective-permute-start | bytes 22020104 | tf_op jit(solution)/shard_map/ppermute | solution.py:21
  509.0 3.0 copy-start.3
Sparse Core Ops, SparseCore 0:
  15.6 61.0 all-reduce.2
  267.0 59.3 all-reduce.4
where the time goes:
time: 543 us
  waiting for transfers between devices  424 us (78%)
  matrix products  46.4 us (9%)
  local copies, waits for them, and re-layouts  27.1 us (5%)
  other arithmetic  25.2 us (5%)
  between operations  16 us (3%)
    ppermute x2, waiting for transfers between devices, partner(): return lax.ppermute(block, axis, route)  313 us
    psum x2, waiting for transfers between devices, on_device(): outputs = lax.psum(terms.astype(jnp.bfloat16), 'tensor').astype(jnp.float32)  111 us
    dot_general x2, matrix products, contract_rows(): lax.dot_general(left, right, (((0,), (0,)), ((), ())), preferred_element_...  24.3 us
    dot_general x2, matrix products, on_device(): jnp.dot(hidden_rows, weight_block, preferred_element_type=jnp.float32)  22.1 us
    unnamed x17, local copies, waits for them, and re-layouts  16 us
    broadcast_in_dim x1, other arithmetic, on_device(): return weight_block[None]  13.3 us
  transfers between devices with their start and end apart: 4, of which 4 were waited for; matrix products, arithmetic and copies ran while one was open for 2% of the time, Pallas kernels for 0%

commit v1 on v0

v1 whole, which is shorter than its diff:
```python
import jax
import jax.numpy as jnp
from jax import lax
from jax.experimental import pallas as pl
from jax.experimental.pallas import tpu as pltpu
from jax.sharding import PartitionSpec as P

FF = 7168
EPS = 1e-05
LEARN_RATE = 0.5
FACTOR = FF ** (-0.5)
CHUNKS = 7
GROUPS = tuple((i, 1) for i in range(CHUNKS))


def mm(left, right):
    return jnp.dot(left, right, preferred_element_type=jnp.float32)


def mm_rows(left, right):
    return lax.dot_general(left, right, (((0,), (0,)), ((), ())), preferred_element_type=jnp.float32)


def meet(*values):
    return lax.optimization_barrier(values)


def call(body, grid, in_specs, out_specs, out_shape, name, vmem_mib, aliases=None, scratch=()):
    return pl.pallas_call(
        body,
        grid_spec=pltpu.PrefetchScalarGridSpec(
            num_scalar_prefetch=2,
            grid=grid,
            in_specs=in_specs,
            out_specs=out_specs,
            scratch_shapes=list(scratch),
        ),
        out_shape=out_shape,
        input_output_aliases=aliases or {},
        compiler_params=pltpu.CompilerParams(vmem_limit_bytes=vmem_mib * 1024 * 1024),
        cost_estimate=pl.CostEstimate(flops=1, bytes_accessed=1, transcendentals=0),
        name=name,
    )


def on_device(weights, hidden, targets, norm_gain, stragglers):
    replicas, shards = lax.axis_size("replica"), lax.axis_size("tensor")
    tokens, ff = hidden.shape[2], hidden.shape[3]
    features = weights.shape[2]
    half = tokens // 2
    wide = features // 2
    cols = features // 4
    rows = ff // CHUNKS
    deep = ff // 2
    replica = lax.axis_index("replica")
    core = lax.rem(lax.axis_index("tensor"), 2)
    gain = norm_gain.reshape(1, features)
    raw_hidden = hidden
    weights, hidden, targets = (pltpu.with_memory_space_constraint(a, pltpu.HBM) for a in (weights, hidden, targets))
    place = jnp.stack([core, 1 - core]).astype(jnp.int32)
    turn = [place]

    def permute(block, flip_replica, flip_tensor):
        route = [
            (r * shards + t, (r ^ flip_replica) * shards + (t ^ flip_tensor))
            for r in range(replicas)
            for t in range(shards)
        ]
        return lax.ppermute(block, ("replica", "tensor"), route)

    def run(kernel, *args):
        out = kernel(turn[0], *args)
        several = isinstance(out, (list, tuple))
        turn[0], *out = meet(turn[0], *(out if several else [out]))
        return out if several else out[0]

    def grid_block(shape):
        return pl.BlockSpec(shape, lambda n, p, c: (0, n))

    def term_block(index):
        return pl.BlockSpec((rows, cols), lambda n, p, c: (index, n))

    def pair_shapes():
        return [
            jax.ShapeDtypeStruct((half, wide), jnp.bfloat16),
            jax.ShapeDtypeStruct((half, wide), jnp.float32),
        ]

    def split_store(p, total, send, keep, acc):
        acc[...] = total
        keep[...] = acc[pl.ds(pl.multiple_of(p[0] * half, half), half), :]
        send[...] = acc[pl.ds(pl.multiple_of(p[1] * half, half), half), :].astype(send.dtype)

    split_out = [grid_block((half, cols)), grid_block((half, cols))]
    split_scratch = [pltpu.VMEM((tokens, cols), jnp.float32)]

    def forward(side):
        def body(p, c, h, *refs):
            *w, send, keep, acc = refs
            total = sum(mm(h[0, 0, :, i * deep : (i + 1) * deep], w[i][0]) for i in range(2))
            split_store(p, FACTOR * total, send, keep, acc)

        def weight_block(i):
            return pl.BlockSpec((1, deep, cols), lambda n, p, c: (0, i, 2 * side + n))

        return run(
            call(
                body,
                (2,),
                [pl.BlockSpec((1, 1, tokens, ff), lambda n, p, c: (0, 0, 0, 0))]
                + [weight_block(i) for i in range(2)],
                split_out,
                pair_shapes(),
                "forward",
                20,
                scratch=split_scratch,
            ),
            place,
            hidden,
            *[weights] * 2,
        )

    def norm_backward(step, summed, received):
        tile = half // 2
        strip = min(16, tile)

        def body(p, c, s0, s1, r0, r1, t, g, o):
            for i in range(tile // strip):
                span = slice(i * strip, (i + 1) * strip)
                left = s0[span, :].astype(jnp.float32) + r0[span, :].astype(jnp.float32)
                right = s1[span, :].astype(jnp.float32) + r1[span, :].astype(jnp.float32)
                outputs = jnp.concatenate([left, right], axis=1)
                inverse = lax.rsqrt(jnp.mean(outputs * outputs, axis=-1, keepdims=True) + EPS)
                normed = outputs * inverse
                weighted = (normed * g[...] - t[0, 0, span, :].astype(jnp.float32)) * g[...]
                cross = jnp.mean(weighted * normed, axis=-1, keepdims=True)
                o[span, :] = (inverse * (weighted - normed * cross)).astype(o.dtype)

        side = pl.BlockSpec((tile, wide), lambda i, p, c: (i, 0))
        return run(
            call(
                body,
                (2,),
                [side] * 4
                + [
                    pl.BlockSpec((1, 1, tile, features), lambda i, p, c: (0, step, p[0] * 2 + i, 0)),
                    pl.BlockSpec((1, features), lambda i, p, c: (0, 0)),
                ],
                pl.BlockSpec((tile, features), lambda i, p, c: (i, 0)),
                jax.ShapeDtypeStruct((half, features), jnp.bfloat16),
                "norm_backward",
                16,
            ),
            place,
            *summed,
            *received,
            targets,
            gain,
        )

    def update(groups, grad_own, grad_other):
        total = len(groups)

        def body(p, c, *refs):
            go, gx = refs[:2]
            for i in range(total):
                ho, hx, w, o = (refs[2 + j * total + i] for j in range(4))
                grad = mm_rows(ho[0, 0], go[...]) + mm_rows(hx[0, 0], gx[...])
                grad = (FACTOR * grad).astype(jnp.bfloat16).astype(jnp.float32)
                o[...] = (w[0].astype(jnp.float32) - LEARN_RATE * grad).astype(o.dtype)

        def hidden_block(side, at, count):
            return pl.BlockSpec((1, 1, half, count * rows), lambda n, p, c: (0, 0, p[side], at // count))

        def weight_block(at, count):
            return pl.BlockSpec((1, count * rows, cols), lambda n, p, c: (0, at // count, n))

        return run(
            call(
                body,
                (4,),
                [grid_block((half, cols))] * 2
                + [hidden_block(0, *group) for group in groups]
                + [hidden_block(1, *group) for group in groups]
                + [weight_block(*group) for group in groups],
                [grid_block((count * rows, cols)) for _, count in groups],
                [jax.ShapeDtypeStruct((count * rows, features), jnp.bfloat16) for _, count in groups],
                "update",
                24,
            ),
            place,
            grad_own,
            grad_other,
            *[hidden] * (2 * total),
            *[weights] * total,
        )

    def begin(blocks):
        def body(p, c, h, *refs):
            *w, o = refs
            o[...] = sum(
                mm(h[0, 0, :, at * rows : (at + count) * rows], block[...])
                for (at, count), block in zip(GROUPS, w)
            )

        return run(
            call(
                body,
                (4,),
                [pl.BlockSpec((1, 1, tokens, ff), lambda n, p, c: (0, 1, 0, 0))]
                + [grid_block((count * rows, cols)) for _, count in GROUPS[:-1]],
                grid_block((tokens, cols)),
                jax.ShapeDtypeStruct((tokens, features), jnp.float32),
                "begin",
                20,
            ),
            place,
            hidden,
            *blocks,
        )

    def finish(side, begun, block):
        def body(p, c, a, h, w, send, keep, acc):
            split_store(p, FACTOR * (a[...] + mm(h[0, 0], w[...])), send, keep, acc)

        return run(
            call(
                body,
                (2,),
                [
                    pl.BlockSpec((tokens, cols), lambda n, p, c: (0, 2 * side + n)),
                    pl.BlockSpec((1, 1, tokens, rows), lambda n, p, c: (0, 1, 0, CHUNKS - 1)),
                    pl.BlockSpec((rows, cols), lambda n, p, c: (0, 2 * side + n)),
                ],
                split_out,
                pair_shapes(),
                "finish",
                12,
                scratch=split_scratch,
            ),
            place,
            begun,
            hidden,
            block,
        )

    def output_own(grads, own, got):
        def body(p, c, ho, hx, go, gx, *refs):
            o = refs[-1]
            keep = c[0].astype(jnp.bfloat16)
            gos, gxs = go[...] * keep, gx[...] * keep
            for i, (at, count) in enumerate(GROUPS):
                for k in range(count):
                    span = slice((at + k) * rows, (at + k + 1) * rows)
                    part = slice(k * rows, (k + 1) * rows)
                    grad = mm_rows(ho[0, 0, :, span], gos) + mm_rows(hx[0, 0, :, span], gxs)
                    base = c[0] * refs[i][part, :].astype(jnp.float32)
                    base = base + c[1] * refs[len(GROUPS) + i][part, :].astype(jnp.float32)
                    o[0, span, :] = (base - LEARN_RATE * FACTOR * grad).astype(o.dtype)

        blocks = [grid_block((count * rows, cols)) for _, count in GROUPS]
        return run(
            call(
                body,
                (4,),
                [
                    pl.BlockSpec((1, 1, half, ff), lambda n, p, c: (0, 1, p[0], 0)),
                    pl.BlockSpec((1, 1, half, ff), lambda n, p, c: (0, 1, p[1], 0)),
                ]
                + [grid_block((half, cols))] * 2
                + blocks * 2,
                pl.BlockSpec((1, ff, cols), lambda n, p, c: (0, 0, n)),
                jax.ShapeDtypeStruct(weights.shape, weights.dtype),
                "output_own",
                32,
            ),
            coef,
            hidden,
            hidden,
            *grads,
            *own,
            *got,
        )

    def output_far(grads, base):
        def body(p, c, ho, hx, go, gx, b, o):
            take = c[1].astype(jnp.bfloat16)
            gos, gxs = go[...] * take, gx[...] * take
            for i in range(CHUNKS):
                span = slice(i * rows, (i + 1) * rows)
                grad = mm_rows(ho[:, span], gos) + mm_rows(hx[:, span], gxs)
                total = b[0, span, :].astype(jnp.float32) - LEARN_RATE * FACTOR * grad
                o[0, span, :] = total.astype(o.dtype)

        whole = pl.BlockSpec((1, ff, cols), lambda n, p, c: (0, 0, n))
        return run(
            call(
                body,
                (4,),
                [
                    pl.BlockSpec((half, ff), lambda n, p, c: (p[0], 0)),
                    pl.BlockSpec((half, ff), lambda n, p, c: (p[1], 0)),
                ]
                + [grid_block((half, cols))] * 2
                + [whole],
                whole,
                jax.ShapeDtypeStruct(weights.shape, weights.dtype),
                "output_far",
                28,
            ),
            coef,
            borrowed,
            borrowed,
            *grads,
            base,
        )

    def mix(scale_a, a, scale_b, b):
        return (scale_a * a.astype(jnp.float32) + scale_b * b.astype(jnp.float32)).astype(jnp.bfloat16)

    def add(kept, *parts):
        return sum([part.astype(jnp.float32) for part in parts], kept).astype(jnp.bfloat16)

    sent, kept = zip(*[forward(side) for side in range(2)])
    from_core = [permute(block, 0, 1) for block in sent]
    summed = [add(k, f) for k, f in zip(kept, from_core)]
    summed[0], raw_hidden, late = meet(summed[0], raw_hidden, stragglers)
    lone = raw_hidden[0, 1]
    summed[1], lone = meet(summed[1], lone)
    from_z = [permute(block, 0, 2) for block in summed]
    borrowed = permute(lone, 2, 0)

    def pair(step, low, high):
        count = lax.dynamic_index_in_dim(late[step], low, keepdims=False)
        count += lax.dynamic_index_in_dim(late[step], high, keepdims=False)
        return jnp.where(count == 0, jnp.float32(0.5), jnp.float32(0.0))

    near, mine = pair(0, replica, replica ^ 1), pair(1, replica, replica ^ 2)
    coef = jnp.stack([1 - mine, mine])
    from_z[0], near, coef = meet(from_z[0], near, coef)

    grad_own = norm_backward(0, summed, from_z)
    grad_other = permute(grad_own, 0, 1)

    updated = update(GROUPS[:1], grad_own, grad_other)
    updated += update(GROUPS[1:], grad_own, grad_other)
    got = [permute(block, 1, 0) for block in updated]
    averaged, x_got = [], []
    for i in range(len(GROUPS)):
        if i > 1:
            got[i], x_got[i - 2] = meet(got[i], x_got[i - 2])
        elif i == 0:
            got[i], borrowed = meet(got[i], borrowed)
        averaged.append(mix(1 - near, updated[i], near, got[i]))
        x_got.append(permute(averaged[i], 2, 0))

    begun = begin(averaged[:-1])
    sent, kept = zip(*[finish(side, begun, averaged[-1]) for side in range(2)])
    from_core = [permute(block, 0, 1) for block in sent]
    summed = [add(k, f) for k, f in zip(kept, from_core)]
    summed[1], x_got[-2] = meet(summed[1], x_got[-2])
    from_z = [permute(block, 0, 2) for block in summed]
    *from_z, x_got[-1] = meet(*from_z, x_got[-1])
    next_own = norm_backward(1, summed, from_z)
    next_other = permute(next_own, 0, 1)
    far_own = permute(next_own, 2, 0)
    base = output_own((next_own, next_other), averaged, x_got)
    base = pltpu.with_memory_space_constraint(base, pltpu.HBM)
    base, far_own = meet(base, far_own)
    far_other = permute(far_own, 0, 1)
    return output_far((far_own, far_other), base)


def solution(mesh):
    placed = (
        P("replica", "tensor", None),
        P("replica", None, None, "tensor"),
        P("replica", None, None, None),
        P(),
        P(),
    )
    return jax.shard_map(
        on_device,
        mesh=mesh,
        in_specs=placed,
        out_specs=P("replica", "tensor", None),
        check_vma=False,
    )
```

time: 543 us -> 288 us (0.53)
  waiting for transfers between devices: 424 us -> 176 us
  Pallas kernels: 0 us -> 59.3 us
  matrix products: 46.4 us -> 0 us
  starting transfers between devices: 3.81 us -> 40.9 us
  local copies, waits for them, and re-layouts: 27.1 us -> 3.24 us
  other arithmetic: 25.2 us -> 5.59 us
  between operations: 16 us -> 2.66 us
    ppermute x2 -> x27, waiting for transfers between devices: 313 us -> 176 us  [permute(): return lax.ppermute(block, ('replica', 'tensor'), route)]
    psum x2 -> x0, waiting for transfers between devices: 111 us -> none  [on_device(): outputs = lax.psum(terms.astype(jnp.bfloat16), 'tensor').astype(jnp.float32)]
    pallas_call x0 -> x11, Pallas kernels: none -> 59.3 us  [run(): out = kernel(turn[0], *args)]
    dot_general x4 -> x0, matrix products: 46.4 us -> none  [the longest x2 24.3 us: contract_rows(): lax.dot_general(left, right, (((0,), (0,)), ((), ())), preferred_element_...]
    ppermute x2 -> x27, starting transfers between devices: 3.77 us -> 40.9 us  [permute(): return lax.ppermute(block, ('replica', 'tensor'), route)]
    unnamed x17 -> x10, local copies, waits for them, and re-layouts: 16 us -> 1.24 us
    broadcast_in_dim x1 -> x0, other arithmetic: 13.3 us -> none  [on_device(): return weight_block[None]]
    reduce_sum x4 -> x0, other arithmetic: 11.8 us -> none  [the longest x2 7.35 us: norm_backward(): cross_mean = jnp.mean(weighted * normed, axis=-1, keepdims=True)]
  transfers between devices with their start and end apart: 4 -> 27, of which waited for: 4 -> 18; matrix products, arithmetic and copies ran while one was open for 2% -> 3% of each run, Pallas kernels for 0% -> 14%
where the time goes in v1:
time: 288 us
  waiting for transfers between devices  176 us (61%)
  Pallas kernels  59.3 us (21%)
  starting transfers between devices  40.9 us (14%)
  other arithmetic  5.59 us (2%)
  local copies, waits for them, and re-layouts  3.24 us (1%)
    ppermute x27, waiting for transfers between devices, permute(): return lax.ppermute(block, ('replica', 'tensor'), route)  176 us
    pallas_call x11, Pallas kernels, run(): out = kernel(turn[0], *args)  59.3 us
    ppermute x27, starting transfers between devices, permute(): return lax.ppermute(block, ('replica', 'tensor'), route)  40.9 us
  transfers between devices with their start and end apart: 27, of which 18 were waited for; matrix products, arithmetic and copies ran while one was open for 3% of the time, Pallas kernels for 14%

profile of v1, /device:TPU:1, one launch (start us, length us, event | category | flops | bytes accessed | tf_op | source)
XLA Modules:
  0.0 287.5 jit_solution(12088316833146583666)
XLA Ops:
  0.1 5.4 %forward.2 = (bf16[256,1024]{1,0:T(8,128)(2,1)S(1)}, f32[256,1024]{1,0:T(8,128)S(1)}) custom-call(s32[2]{0:T(128)S(1)} %pad_add_fusion.p.c, s32[2]{0:T(128)S(1)} %pad_add_fusion.p.c, bf16[1,2,512,1792]{3,2,1,0:T(8,128)(2,1)} %hx.1, bf16[1,1792,2048]{2,1,0:T(8,128)(2,1)} %refs_19_.1, bf16[1,1792,2048]{2,1,0:T(8,128)(2,1)} %refs_19_.1), custom_call_target="tpu_custom_call" | custom-call | flops 1 | bytes 1 | tf_op jit(solution)/shard_map/forward/pallas_call | solution.py:72
  7.0 5.8 %forward.3 = (bf16[256,1024]{1,0:T(8,128)(2,1)S(1)}, f32[256,1024]{1,0:T(8,128)S(1)}) custom-call(s32[2]{0:T(128)S(1)} %pad_add_fusion.p.c, s32[2]{0:T(128)S(1)} %pad_add_fusion.p.c, bf16[1,2,512,1792]{3,2,1,0:T(8,128)(2,1)} %hx.1, bf16[1,1792,2048]{2,1,0:T(8,128)(2,1)} %refs_19_.1, bf16[1,1792,2048]{2,1,0:T(8,128)(2,1)} %refs_19_.1), custom_call_target="tpu_custom_call" | custom-call | flops 1 | bytes 1 | tf_op jit(solution)/shard_map/forward/pallas_call | solution.py:72
  19.9 6.8 %collective-permute-done.2.r0 = bf16[256,1024]{1,0:T(8,128)(2,1)S(1)} collective-permute-done((bf16[256,1024]{1,0:T(8,128)(2,1)S(1)}, bf16[256,1024]{1,0:T(8,128)(2,1)S(1)}, u32[]{:S(2)}, u32[]{:S(2)}) %collective-permute-start.2) | collective-permute-done | bytes 524320 | tf_op jit(solution)/shard_map/ppermute | solution.py:69
  26.7 11.2 %collective-permute-done.3.r1 = bf16[256,1024]{1,0:T(8,128)(2,1)S(1)} collective-permute-done((bf16[256,1024]{1,0:T(8,128)(2,1)S(1)}, bf16[256,1024]{1,0:T(8,128)(2,1)S(1)}, u32[]{:S(2)}, u32[]{:S(2)}) %collective-permute-start.3) | collective-permute-done | bytes 524320 | tf_op jit(solution)/shard_map/ppermute | solution.py:69
  44.2 4.8 %update.2 = bf16[256,2048]{1,0:T(8,128)(2,1)} custom-call(s32[2]{0:T(128)S(1)} %pad_add_fusion.p.c, s32[2]{0:T(128)S(1)} %pad_add_fusion.p.c, bf16[256,2048]{1,0:T(8,128)(2,1)S(1)} %norm_backward.2.refs_0_, bf16[256,2048]{1,0:T(8,128)(2,1)S(1)} %collective-permute-done.4.refs_1_, bf16[1,2,512,1792]{3,2,1,0:T(8,128)(2,1)} %hx.1, ...), custom_call_target="tpu_custom_call" | custom-call | flops 1 | bytes 1 | tf_op jit(solution)/shard_map/update/pallas_call | solution.py:72
  49.0 3.4 %collective-permute-start.5 = (bf16[256,2048]{1,0:T(8,128)(2,1)}, bf16[256,2048]{1,0:T(8,128)(2,1)}, u32[]{:S(2)}, u32[]{:S(2)}) collective-permute-start(bf16[256,2048]{1,0:T(8,128)(2,1)} %update.2), channel_id=1, source_target_pairs={{0,4},{1,5},{2,6},{3,7},{4,0},{5,1},{6,2},{7,3},{8,12},{9,13},{10,... | collective-permute-start | bytes 3145736 | tf_op jit(solution)/shard_map/ppermute | solution.py:69
  53.7 7.9 %update.3 = (bf16[256,2048]{1,0:T(8,128)(2,1)S(1)}, bf16[256,2048]{1,0:T(8,128)(2,1)S(1)}, bf16[256,2048]{1,0:T(8,128)(2,1)S(1)}, bf16[256,2048]{1,0:T(8,128)(2,...) custom-call(s32[2]{0:T(128)S(1)} %pad_add_fusion.p.c, s32[2]{0:T(128)S(1)} %pad_add_fusion.p.c, ...), custom_call_target="tpu_custom_call" | custom-call | flops 1 | bytes 1 | tf_op jit(solution)/shard_map/update/pallas_call | solution.py:72
  61.7 3.0 %collective-permute-start.8 = (bf16[256,2048]{1,0:T(8,128)(2,1)S(1)}, bf16[256,2048]{1,0:T(8,128)(2,1)S(1)}, u32[]{:S(2)}, u32[]{:S(2)}) collective-permute-start(bf16[256,2048]{1,0:T(8,128)(2,1)S(1)} %get-tuple-element.106), channel_id=1, source_target_pairs={{0,4},{1,5},{2,6},{3,7},{4,0},{5,1},{6,2},{7,3},{8,12},{9,13},{10,... | collective-permute-start | bytes 3145736 | tf_op jit(solution)/shard_map/ppermute | solution.py:69
  64.6 19.0 %collective-permute-done.6.ho.hx = bf16[512,1792]{1,0:T(8,128)(2,1)S(1)} collective-permute-done((bf16[512,1792]{1,0:T(8,128)(2,1)}, bf16[512,1792]{1,0:T(8,128)(2,1)S(1)}, u32[]{:S(2)}, u32[]{:S(2)}) %collective-permute-start.6) | collective-permute-done | bytes 1835040 | tf_op jit(solution)/shard_map/ppermute | solution.py:69
  87.0 3.4 %collective-permute-start.10 = (bf16[256,2048]{1,0:T(8,128)(2,1)S(1)}, bf16[256,2048]{1,0:T(8,128)(2,1)S(1)}, u32[]{:S(2)}, u32[]{:S(2)}) collective-permute-start(bf16[256,2048]{1,0:T(8,128)(2,1)S(1)} %get-tuple-element.108), channel_id=1, source_target_pairs={{0,4},{1,5},{2,6},{3,7},{4,0},{5,1},{6,2},{7,3},{8,12},{9,13},{10,... | collective-permute-start | bytes 3145736 | tf_op jit(solution)/shard_map/ppermute | solution.py:69
  90.4 7.9 %collective-permute-done.7 = bf16[256,2048]{1,0:T(8,128)(2,1)S(1)} collective-permute-done((bf16[256,2048]{1,0:T(8,128)(2,1)S(1)}, bf16[256,2048]{1,0:T(8,128)(2,1)S(1)}, u32[]{:S(2)}, u32[]{:S(2)}) %collective-permute-start.7) | collective-permute-done | bytes 1048608 | tf_op jit(solution)/shard_map/ppermute | solution.py:69
  102.7 18.1 %collective-permute-done.8 = bf16[256,2048]{1,0:T(8,128)(2,1)S(1)} collective-permute-done((bf16[256,2048]{1,0:T(8,128)(2,1)S(1)}, bf16[256,2048]{1,0:T(8,128)(2,1)S(1)}, u32[]{:S(2)}, u32[]{:S(2)}) %collective-permute-start.8) | collective-permute-done | bytes 1048608 | tf_op jit(solution)/shard_map/ppermute | solution.py:69
  125.2 18.1 %collective-permute-done.10 = bf16[256,2048]{1,0:T(8,128)(2,1)S(1)} collective-permute-done((bf16[256,2048]{1,0:T(8,128)(2,1)S(1)}, bf16[256,2048]{1,0:T(8,128)(2,1)S(1)}, u32[]{:S(2)}, u32[]{:S(2)}) %collective-permute-start.10) | collective-permute-done | bytes 1048608 | tf_op jit(solution)/shard_map/ppermute | solution.py:69
  147.7 18.1 %collective-permute-done.12 = bf16[256,2048]{1,0:T(8,128)(2,1)S(1)} collective-permute-done((bf16[256,2048]{1,0:T(8,128)(2,1)S(1)}, bf16[256,2048]{1,0:T(8,128)(2,1)S(1)}, u32[]{:S(2)}, u32[]{:S(2)}) %collective-permute-start.12) | collective-permute-done | bytes 1048608 | tf_op jit(solution)/shard_map/ppermute | solution.py:69
  167.5 20.7 %collective-permute-done.14 = bf16[256,2048]{1,0:T(8,128)(2,1)S(1)} collective-permute-done((bf16[256,2048]{1,0:T(8,128)(2,1)S(1)}, bf16[256,2048]{1,0:T(8,128)(2,1)S(1)}, u32[]{:S(2)}, u32[]{:S(2)}) %collective-permute-start.14) | collective-permute-done | bytes 1048608 | tf_op jit(solution)/shard_map/ppermute | solution.py:69
  190.2 6.6 %begin.1.a = f32[512,2048]{1,0:T(8,128)S(1)} custom-call(s32[2]{0:T(128)S(1)} %pad_add_fusion.p.c, s32[2]{0:T(128)S(1)} %pad_add_fusion.p.c, bf16[1,2,512,1792]{3,2,1,0:T(8,128)(2,1)} %hx.1, bf16[256,2048]{1,0:T(8,128)(2,1)S(1)} %add_convert_fusion.6.refs_0_, bf16[256,2048]{1,0:T(8,128)(2,1)S(1)} %add_convert_fusion.5.refs_1_, ...), custom_call_target="tpu_custom_call" | custom-call | flops 1 | bytes 1 | tf_op jit(solution)/shard_map/begin/pallas_call | solution.py:72
  196.8 13.9 %collective-permute-done.16 = bf16[256,2048]{1,0:T(8,128)(2,1)S(1)} collective-permute-done((bf16[256,2048]{1,0:T(8,128)(2,1)S(1)}, bf16[256,2048]{1,0:T(8,128)(2,1)S(1)}, u32[]{:S(2)}, u32[]{:S(2)}) %collective-permute-start.16) | collective-permute-done | bytes 1048608 | tf_op jit(solution)/shard_map/ppermute | solution.py:69
  218.8 3.2 %collective-permute-done.20.refs_12_ = bf16[256,2048]{1,0:T(8,128)(2,1)S(1)} collective-permute-done((bf16[256,2048]{1,0:T(8,128)(2,1)S(1)}, bf16[256,2048]{1,0:T(8,128)(2,1)S(1)}, u32[]{:S(2)}, u32[]{:S(2)}) %collective-permute-start.20) | collective-permute-done | bytes 1048608 | tf_op jit(solution)/shard_map/ppermute | solution.py:69
  223.7 8.6 %collective-permute-done.22.r1 = bf16[256,1024]{1,0:T(8,128)(2,1)S(1)} collective-permute-done((bf16[256,1024]{1,0:T(8,128)(2,1)S(1)}, bf16[256,1024]{1,0:T(8,128)(2,1)S(1)}, u32[]{:S(2)}, u32[]{:S(2)}) %collective-permute-start.22) | collective-permute-done | bytes 524320 | tf_op jit(solution)/shard_map/ppermute | solution.py:69
  232.2 11.2 %collective-permute-done.21.r0 = bf16[256,1024]{1,0:T(8,128)(2,1)S(1)} collective-permute-done((bf16[256,1024]{1,0:T(8,128)(2,1)S(1)}, bf16[256,1024]{1,0:T(8,128)(2,1)S(1)}, u32[]{:S(2)}, u32[]{:S(2)}) %collective-permute-start.21) | collective-permute-done | bytes 524320 | tf_op jit(solution)/shard_map/ppermute | solution.py:69
  247.3 3.2 %collective-permute-start.24 = (bf16[256,2048]{1,0:T(8,128)(2,1)S(1)}, bf16[256,2048]{1,0:T(8,128)(2,1)S(1)}, u32[]{:S(2)}, u32[]{:S(2)}) collective-permute-start(bf16[256,2048]{1,0:T(8,128)(2,1)S(1)} %norm_backward.3.go), channel_id=1, source_target_pairs={{0,1},{1,0},{2,3},{3,2},{4,5},{5,4},{6,7},{7,6},{8,9},{9,8},{10,11... | collective-permute-start | bytes 3145736 | tf_op jit(solution)/shard_map/ppermute | solution.py:69
  252.7 9.1 %output_own.1.b = bf16[1,1792,2048]{2,1,0:T(8,128)(2,1)} custom-call(s32[2]{0:T(128)S(1)} %pad_add_fusion.p.c, f32[2]{0:T(128)S(1)} %pad_maximum_fusion.c, bf16[1,2,512,1792]{3,2,1,0:T(8,128)(2,1)} %hx.1, bf16[1,2,512,1792]{3,2,1,0:T(8,128)(2,1)} %hx.1, bf16[256,2048]{1,0:T(8,128)(2,1)S(1)} %norm_backward.3.go, ...), custom_call_target="tpu_custom_call" | custom-call | flops 1 | bytes 1 | tf_op jit(solution)/shard_map/output_own/pallas_call | solution.py:72
  261.8 13.4 %collective-permute-done.25.go = bf16[256,2048]{1,0:T(8,128)(2,1)S(1)} collective-permute-done((bf16[256,2048]{1,0:T(8,128)(2,1)S(1)}, bf16[256,2048]{1,0:T(8,128)(2,1)S(1)}, u32[]{:S(2)}, u32[]{:S(2)}) %collective-permute-start.25) | collective-permute-done | bytes 1048608 | tf_op jit(solution)/shard_map/ppermute | solution.py:69
  278.3 9.2 %output_far.1 = bf16[1,1792,2048]{2,1,0:T(8,128)(2,1)} custom-call(s32[2]{0:T(128)S(1)} %pad_add_fusion.p.c, f32[2]{0:T(128)S(1)} %pad_maximum_fusion.c, bf16[512,1792]{1,0:T(8,128)(2,1)S(1)} %collective-permute-done.6.ho.hx, bf16[512,1792]{1,0:T(8,128)(2,1)S(1)} %collective-permute-done.6.ho.hx, bf16[256,2048]{1,0:T(8,128)(2,1)S(1)} %collective-permute-done.25.go, ...), custom_call_target="tpu_custom_call" | custom-call | flops 1 | bytes 1 | tf_op jit(solution)/shard_map/output_far/pallas_call | solution.py:72
  (67 shorter events, 52.9 us)
Async XLA Ops:
  5.5 7.4 %collective-permute-start = (bf16[256,1024]{1,0:T(8,128)(2,1)S(1)}, bf16[256,1024]{1,0:T(8,128)(2,1)S(1)}, u32[]{:S(2)}, u32[]{:S(2)}) collective-permute-start(bf16[256,1024]{1,0:T(8,128)(2,1)S(1)} %get-tuple-element.83), channel_id=1, source_target_pairs={{0,1},{1,0},{2,3},{3,2},{4,5},{5,4},{6,7},{7,6},{8,9},{9,8},{10,11... | collective-permute-start | bytes 1572872 | tf_op jit(solution)/shard_map/ppermute | solution.py:69
  12.8 3.5 %collective-permute-start.1 = (bf16[256,1024]{1,0:T(8,128)(2,1)S(1)}, bf16[256,1024]{1,0:T(8,128)(2,1)S(1)}, u32[]{:S(2)}, u32[]{:S(2)}) collective-permute-start(bf16[256,1024]{1,0:T(8,128)(2,1)S(1)} %get-tuple-element.86), channel_id=1, source_target_pairs={{0,1},{1,0},{2,3},{3,2},{4,5},{5,4},{6,7},{7,6},{8,9},{9,8},{10,11... | collective-permute-start | bytes 1572872 | tf_op jit(solution)/shard_map/ppermute | solution.py:69
  13.1 13.6 %collective-permute-start.2 = (bf16[256,1024]{1,0:T(8,128)(2,1)S(1)}, bf16[256,1024]{1,0:T(8,128)(2,1)S(1)}, u32[]{:S(2)}, u32[]{:S(2)}) collective-permute-start(bf16[256,1024]{1,0:T(8,128)(2,1)S(1)} %add_convert_fusion.10.s0), channel_id=1, source_target_pairs={{0,2},{1,3},{2,0},{3,1},{4,6},{5,7},{6,4},{7,5},{8,10},{9,11},{10,... | collective-permute-start | bytes 1572872 | tf_op jit(solution)/shard_map/ppermute | solution.py:69
  16.4 21.6 %collective-permute-start.3 = (bf16[256,1024]{1,0:T(8,128)(2,1)S(1)}, bf16[256,1024]{1,0:T(8,128)(2,1)S(1)}, u32[]{:S(2)}, u32[]{:S(2)}) collective-permute-start(bf16[256,1024]{1,0:T(8,128)(2,1)S(1)} %add_convert_fusion.9.s1), channel_id=1, source_target_pairs={{0,2},{1,3},{2,0},{3,1},{4,6},{5,7},{6,4},{7,5},{8,10},{9,11},{10,... | collective-permute-start | bytes 1572872 | tf_op jit(solution)/shard_map/ppermute | solution.py:69
  41.9 41.8 %collective-permute-start.6 = (bf16[512,1792]{1,0:T(8,128)(2,1)}, bf16[512,1792]{1,0:T(8,128)(2,1)S(1)}, u32[]{:S(2)}, u32[]{:S(2)}) collective-permute-start(bf16[512,1792]{1,0:T(8,128)(2,1)} %slice_bitcast_fusion), channel_id=1, source_target_pairs={{0,8},{1,9},{2,10},{3,11},{4,12},{5,13},{6,14},{7,15},{8,0},{9,1},... | collective-permute-start | bytes 5505032 | tf_op jit(solution)/shard_map/ppermute | solution.py:69
  49.0 34.7 %collective-permute-start.5 = (bf16[256,2048]{1,0:T(8,128)(2,1)}, bf16[256,2048]{1,0:T(8,128)(2,1)}, u32[]{:S(2)}, u32[]{:S(2)}) collective-permute-start(bf16[256,2048]{1,0:T(8,128)(2,1)} %update.2), channel_id=1, source_target_pairs={{0,4},{1,5},{2,6},{3,7},{4,0},{5,1},{6,2},{7,3},{8,12},{9,13},{10,... | collective-permute-start | bytes 3145736 | tf_op jit(solution)/shard_map/ppermute | solution.py:69
  61.6 36.8 %collective-permute-start.7 = (bf16[256,2048]{1,0:T(8,128)(2,1)S(1)}, bf16[256,2048]{1,0:T(8,128)(2,1)S(1)}, u32[]{:S(2)}, u32[]{:S(2)}) collective-permute-start(bf16[256,2048]{1,0:T(8,128)(2,1)S(1)} %get-tuple-element.105), channel_id=1, source_target_pairs={{0,4},{1,5},{2,6},{3,7},{4,0},{5,1},{6,2},{7,3},{8,12},{9,13},{10,... | collective-permute-start | bytes 3145736 | tf_op jit(solution)/shard_map/ppermute | solution.py:69
  61.7 59.1 %collective-permute-start.8 = (bf16[256,2048]{1,0:T(8,128)(2,1)S(1)}, bf16[256,2048]{1,0:T(8,128)(2,1)S(1)}, u32[]{:S(2)}, u32[]{:S(2)}) collective-permute-start(bf16[256,2048]{1,0:T(8,128)(2,1)S(1)} %get-tuple-element.106), channel_id=1, source_target_pairs={{0,4},{1,5},{2,6},{3,7},{4,0},{5,1},{6,2},{7,3},{8,12},{9,13},{10,... | collective-permute-start | bytes 3145736 | tf_op jit(solution)/shard_map/ppermute | solution.py:69
  85.7 35.1 %collective-permute-start.9 = (bf16[256,2048]{1,0:T(8,128)(2,1)S(1)}, bf16[256,2048]{1,0:T(8,128)(2,1)S(1)}, u32[]{:S(2)}, u32[]{:S(2)}) collective-permute-start(bf16[256,2048]{1,0:T(8,128)(2,1)S(1)} %add_convert_fusion.6.refs_0_), channel_id=1, source_target_pairs={{0,8},{1,9},{2,10},{3,11},{4,12},{5,13},{6,14},{7,15},{8,0},{9,1},... | collective-permute-start | bytes 3145736 | tf_op jit(solution)/shard_map/ppermute | solution.py:69
  87.0 56.3 %collective-permute-start.10 = (bf16[256,2048]{1,0:T(8,128)(2,1)S(1)}, bf16[256,2048]{1,0:T(8,128)(2,1)S(1)}, u32[]{:S(2)}, u32[]{:S(2)}) collective-permute-start(bf16[256,2048]{1,0:T(8,128)(2,1)S(1)} %get-tuple-element.108), channel_id=1, source_target_pairs={{0,4},{1,5},{2,6},{3,7},{4,0},{5,1},{6,2},{7,3},{8,12},{9,13},{10,... | collective-permute-start | bytes 3145736 | tf_op jit(solution)/shard_map/ppermute | solution.py:69
  98.8 44.5 %collective-permute-start.11 = (bf16[256,2048]{1,0:T(8,128)(2,1)S(1)}, bf16[256,2048]{1,0:T(8,128)(2,1)S(1)}, u32[]{:S(2)}, u32[]{:S(2)}) collective-permute-start(bf16[256,2048]{1,0:T(8,128)(2,1)S(1)} %add_convert_fusion.5.refs_1_), channel_id=1, source_target_pairs={{0,8},{1,9},{2,10},{3,11},{4,12},{5,13},{6,14},{7,15},{8,0},{9,1},... | collective-permute-start | bytes 3145736 | tf_op jit(solution)/shard_map/ppermute | solution.py:69
  100.1 65.7 %collective-permute-start.12 = (bf16[256,2048]{1,0:T(8,128)(2,1)S(1)}, bf16[256,2048]{1,0:T(8,128)(2,1)S(1)}, u32[]{:S(2)}, u32[]{:S(2)}) collective-permute-start(bf16[256,2048]{1,0:T(8,128)(2,1)S(1)} %get-tuple-element.110), channel_id=1, source_target_pairs={{0,4},{1,5},{2,6},{3,7},{4,0},{5,1},{6,2},{7,3},{8,12},{9,13},{10,... | collective-permute-start | bytes 3145736 | tf_op jit(solution)/shard_map/ppermute | solution.py:69
  121.3 44.5 %collective-permute-start.13 = (bf16[256,2048]{1,0:T(8,128)(2,1)S(1)}, bf16[256,2048]{1,0:T(8,128)(2,1)S(1)}, u32[]{:S(2)}, u32[]{:S(2)}) collective-permute-start(bf16[256,2048]{1,0:T(8,128)(2,1)S(1)} %add_convert_fusion.4.refs_2_), channel_id=1, source_target_pairs={{0,8},{1,9},{2,10},{3,11},{4,12},{5,13},{6,14},{7,15},{8,0},{9,1},... | collective-permute-start | bytes 3145736 | tf_op jit(solution)/shard_map/ppermute | solution.py:69
  122.6 65.7 %collective-permute-start.14 = (bf16[256,2048]{1,0:T(8,128)(2,1)S(1)}, bf16[256,2048]{1,0:T(8,128)(2,1)S(1)}, u32[]{:S(2)}, u32[]{:S(2)}) collective-permute-start(bf16[256,2048]{1,0:T(8,128)(2,1)S(1)} %get-tuple-element.112), channel_id=1, source_target_pairs={{0,4},{1,5},{2,6},{3,7},{4,0},{5,1},{6,2},{7,3},{8,12},{9,13},{10,... | collective-permute-start | bytes 3145736 | tf_op jit(solution)/shard_map/ppermute | solution.py:69
  143.7 44.5 %collective-permute-start.15 = (bf16[256,2048]{1,0:T(8,128)(2,1)S(1)}, bf16[256,2048]{1,0:T(8,128)(2,1)S(1)}, u32[]{:S(2)}, u32[]{:S(2)}) collective-permute-start(bf16[256,2048]{1,0:T(8,128)(2,1)S(1)} %add_convert_fusion.3.refs_3_), channel_id=1, source_target_pairs={{0,8},{1,9},{2,10},{3,11},{4,12},{5,13},{6,14},{7,15},{8,0},{9,1},... | collective-permute-start | bytes 3145736 | tf_op jit(solution)/shard_map/ppermute | solution.py:69
  145.0 65.7 %collective-permute-start.16 = (bf16[256,2048]{1,0:T(8,128)(2,1)S(1)}, bf16[256,2048]{1,0:T(8,128)(2,1)S(1)}, u32[]{:S(2)}, u32[]{:S(2)}) collective-permute-start(bf16[256,2048]{1,0:T(8,128)(2,1)S(1)} %get-tuple-element.116), channel_id=1, source_target_pairs={{0,4},{1,5},{2,6},{3,7},{4,0},{5,1},{6,2},{7,3},{8,12},{9,13},{10,... | collective-permute-start | bytes 3145736 | tf_op jit(solution)/shard_map/ppermute | solution.py:69
  166.2 44.5 %collective-permute-start.17 = (bf16[256,2048]{1,0:T(8,128)(2,1)S(1)}, bf16[256,2048]{1,0:T(8,128)(2,1)S(1)}, u32[]{:S(2)}, u32[]{:S(2)}) collective-permute-start(bf16[256,2048]{1,0:T(8,128)(2,1)S(1)} %add_convert_fusion.2.refs_4_), channel_id=1, source_target_pairs={{0,8},{1,9},{2,10},{3,11},{4,12},{5,13},{6,14},{7,15},{8,0},{9,1},... | collective-permute-start | bytes 3145736 | tf_op jit(solution)/shard_map/ppermute | solution.py:69
  188.7 33.3 %collective-permute-start.20 = (bf16[256,2048]{1,0:T(8,128)(2,1)S(1)}, bf16[256,2048]{1,0:T(8,128)(2,1)S(1)}, u32[]{:S(2)}, u32[]{:S(2)}) collective-permute-start(bf16[256,2048]{1,0:T(8,128)(2,1)S(1)} %add_convert_fusion.1.refs_5_), channel_id=1, source_target_pairs={{0,8},{1,9},{2,10},{3,11},{4,12},{5,13},{6,14},{7,15},{8,0},{9,1},... | collective-permute-start | bytes 3145736 | tf_op jit(solution)/shard_map/ppermute | solution.py:69
  217.1 6.3 %collective-permute-start.18 = (bf16[256,1024]{1,0:T(8,128)(2,1)S(1)}, bf16[256,1024]{1,0:T(8,128)(2,1)S(1)}, u32[]{:S(2)}, u32[]{:S(2)}) collective-permute-start(bf16[256,1024]{1,0:T(8,128)(2,1)S(1)} %get-tuple-element.125), channel_id=1, source_target_pairs={{0,1},{1,0},{2,3},{3,2},{4,5},{5,4},{6,7},{7,6},{8,9},{9,8},{10,11... | collective-permute-start | bytes 1572872 | tf_op jit(solution)/shard_map/ppermute | solution.py:69
  217.2 27.2 %collective-permute-start.23 = (bf16[256,2048]{1,0:T(8,128)(2,1)S(1)}, bf16[256,2048]{1,0:T(8,128)(2,1)S(1)}, u32[]{:S(2)}, u32[]{:S(2)}) collective-permute-start(bf16[256,2048]{1,0:T(8,128)(2,1)S(1)} %add_convert_fusion.w.refs_6_), channel_id=1, source_target_pairs={{0,8},{1,9},{2,10},{3,11},{4,12},{5,13},{6,14},{7,15},{8,0},{9,1},... | collective-permute-start | bytes 3145736 | tf_op jit(solution)/shard_map/ppermute | solution.py:69
  222.0 10.3 %collective-permute-start.22 = (bf16[256,1024]{1,0:T(8,128)(2,1)S(1)}, bf16[256,1024]{1,0:T(8,128)(2,1)S(1)}, u32[]{:S(2)}, u32[]{:S(2)}) collective-permute-start(bf16[256,1024]{1,0:T(8,128)(2,1)S(1)} %add_convert_fusion.7.s1), channel_id=1, source_target_pairs={{0,2},{1,3},{2,0},{3,1},{4,6},{5,7},{6,4},{7,5},{8,10},{9,11},{10,... | collective-permute-start | bytes 1572872 | tf_op jit(solution)/shard_map/ppermute | solution.py:69
  223.6 19.9 %collective-permute-start.21 = (bf16[256,1024]{1,0:T(8,128)(2,1)S(1)}, bf16[256,1024]{1,0:T(8,128)(2,1)S(1)}, u32[]{:S(2)}, u32[]{:S(2)}) collective-permute-start(bf16[256,1024]{1,0:T(8,128)(2,1)S(1)} %add_convert_fusion.8.s0), channel_id=1, source_target_pairs={{0,2},{1,3},{2,0},{3,1},{4,6},{5,7},{6,4},{7,5},{8,10},{9,11},{10,... | collective-permute-start | bytes 1572872 | tf_op jit(solution)/shard_map/ppermute | solution.py:69
  247.3 5.5 %collective-permute-start.24 = (bf16[256,2048]{1,0:T(8,128)(2,1)S(1)}, bf16[256,2048]{1,0:T(8,128)(2,1)S(1)}, u32[]{:S(2)}, u32[]{:S(2)}) collective-permute-start(bf16[256,2048]{1,0:T(8,128)(2,1)S(1)} %norm_backward.3.go), channel_id=1, source_target_pairs={{0,1},{1,0},{2,3},{3,2},{4,5},{5,4},{6,7},{7,6},{8,9},{9,8},{10,11... | collective-permute-start | bytes 3145736 | tf_op jit(solution)/shard_map/ppermute | solution.py:69
  250.4 24.7 %collective-permute-start.25 = (bf16[256,2048]{1,0:T(8,128)(2,1)S(1)}, bf16[256,2048]{1,0:T(8,128)(2,1)S(1)}, u32[]{:S(2)}, u32[]{:S(2)}) collective-permute-start(bf16[256,2048]{1,0:T(8,128)(2,1)S(1)} %norm_backward.3.go), channel_id=1, source_target_pairs={{0,8},{1,9},{2,10},{3,11},{4,12},{5,13},{6,14},{7,15},{8,0},{9,1},... | collective-permute-start | bytes 3145736 | tf_op jit(solution)/shard_map/ppermute | solution.py:69
  (8 other events, 51.6 us)

commit v2 on v1

v2 whole, which is shorter than its diff:
```python
import jax
import jax.numpy as jnp
from jax import lax
from jax.experimental import pallas as pl
from jax.experimental.pallas import tpu as pltpu
from jax.sharding import PartitionSpec as P

FF = 7168
EPS = 1e-05
LEARN_RATE = 0.5
FACTOR = FF ** (-0.5)
UNITS = 14
GROUPS = tuple((2 * i, 2) for i in range(7))


def mm(left, right):
    return jnp.dot(left, right, preferred_element_type=jnp.float32)


def mm_rows(left, right):
    return lax.dot_general(left, right, (((0,), (0,)), ((), ())), preferred_element_type=jnp.float32)


def meet(*values):
    return lax.optimization_barrier(values)


def call(body, grid, in_specs, out_specs, out_shape, name, vmem_mib, aliases=None, scratch=()):
    return pl.pallas_call(
        body,
        grid_spec=pltpu.PrefetchScalarGridSpec(
            num_scalar_prefetch=2,
            grid=grid,
            in_specs=in_specs,
            out_specs=out_specs,
            scratch_shapes=list(scratch),
        ),
        out_shape=out_shape,
        input_output_aliases=aliases or {},
        compiler_params=pltpu.CompilerParams(vmem_limit_bytes=vmem_mib * 1024 * 1024),
        cost_estimate=pl.CostEstimate(flops=1, bytes_accessed=1, transcendentals=0),
        name=name,
    )


def on_device(weights, hidden, targets, norm_gain, stragglers):
    replicas, shards = lax.axis_size("replica"), lax.axis_size("tensor")
    tokens, ff = hidden.shape[2], hidden.shape[3]
    features = weights.shape[2]
    half = tokens // 2
    cols = features // 4
    narrow = features // 8
    unit = ff // UNITS
    deep = ff // 2
    edge = 8 * unit
    replica = lax.axis_index("replica")
    core = lax.rem(lax.axis_index("tensor"), 2)
    near_z = lax.div(lax.axis_index("tensor"), 2)
    quarter = tokens // 4
    gain = norm_gain.reshape(1, features)
    raw_hidden = hidden
    weights, hidden, targets = (pltpu.with_memory_space_constraint(a, pltpu.HBM) for a in (weights, hidden, targets))
    place = jnp.stack([core, 1 - core, near_z, 1 - near_z]).astype(jnp.int32)
    turn = [place]

    def permute(block, flip_replica, flip_tensor):
        route = [
            (r * shards + t, (r ^ flip_replica) * shards + (t ^ flip_tensor))
            for r in range(replicas)
            for t in range(shards)
        ]
        return lax.ppermute(block, ("replica", "tensor"), route)

    def run(kernel, *args):
        out = kernel(turn[0], *args)
        several = isinstance(out, (list, tuple))
        turn[0], *out = meet(turn[0], *(out if several else [out]))
        return out if several else out[0]

    def grid_block(shape):
        return pl.BlockSpec(shape, lambda n, p, c: (0, n))

    def forward():
        def body(p, c, h, w0, w1, send, keep, acc):
            total = mm(h[0, 0, :, :deep], w0[0]) + mm(h[0, 0, :, deep:], w1[0])
            acc[...] = FACTOR * total
            keep[...] = acc[pl.ds(pl.multiple_of(p[0] * half, half), half), :]
            send[...] = acc[pl.ds(pl.multiple_of(p[1] * half, half), half), :].astype(send.dtype)

        return run(
            call(
                body,
                (4,),
                [
                    pl.BlockSpec((1, 1, tokens, ff), lambda n, p, c: (0, 0, 0, 0)),
                    pl.BlockSpec((1, deep, cols), lambda n, p, c: (0, 0, n)),
                    pl.BlockSpec((1, deep, cols), lambda n, p, c: (0, 1, n)),
                ],
                [grid_block((half, cols))] * 2,
                [
                    jax.ShapeDtypeStruct((half, features), jnp.bfloat16),
                    jax.ShapeDtypeStruct((half, features), jnp.float32),
                ],
                "forward",
                14,
                scratch=[pltpu.VMEM((tokens, cols), jnp.float32)],
            ),
            place,
            hidden,
            weights,
            weights,
        )

    def norm_backward(step, summed, received):
        size = summed.shape[0]
        tile = size // 2
        strip = min(16, tile)

        def body(p, c, s, r, t, g, o):
            for i in range(tile // strip):
                span = slice(i * strip, (i + 1) * strip)
                outputs = s[span, :].astype(jnp.float32) + r[span, :].astype(jnp.float32)
                inverse = lax.rsqrt(jnp.mean(outputs * outputs, axis=-1, keepdims=True) + EPS)
                normed = outputs * inverse
                weighted = (normed * g[...] - t[0, 0, span, :].astype(jnp.float32)) * g[...]
                cross = jnp.mean(weighted * normed, axis=-1, keepdims=True)
                o[span, :] = (inverse * (weighted - normed * cross)).astype(o.dtype)

        def target_row(i, p):
            return (p[0] * 2 + p[2] if size == quarter else p[0]) * 2 + i

        block = pl.BlockSpec((tile, features), lambda i, p, c: (i, 0))
        return run(
            call(
                body,
                (2,),
                [
                    block,
                    block,
                    pl.BlockSpec((1, 1, tile, features), lambda i, p, c: (0, step, target_row(i, p), 0)),
                    pl.BlockSpec((1, features), lambda i, p, c: (0, 0)),
                ],
                block,
                jax.ShapeDtypeStruct((size, features), jnp.bfloat16),
                "norm_backward",
                8,
            ),
            place,
            summed,
            received,
            targets,
            gain,
        )

    def update(groups, grad_own, grad_other):
        total = len(groups)

        def body(p, c, *refs):
            go, gx = refs[:2]
            for i in range(total):
                ho, hx, w, o = (refs[2 + j * total + i] for j in range(4))
                grad = mm_rows(ho[0, 0], go[...]) + mm_rows(hx[0, 0], gx[...])
                grad = (FACTOR * grad).astype(jnp.bfloat16).astype(jnp.float32)
                o[...] = (w[0].astype(jnp.float32) - LEARN_RATE * grad).astype(o.dtype)

        def hidden_block(side, at, count):
            return pl.BlockSpec((1, 1, half, count * unit), lambda n, p, c: (0, 0, p[side], at // count))

        def weight_block(at, count):
            return pl.BlockSpec((1, count * unit, cols), lambda n, p, c: (0, at // count, n))

        return run(
            call(
                body,
                (4,),
                [grid_block((half, cols))] * 2
                + [hidden_block(0, *group) for group in groups]
                + [hidden_block(1, *group) for group in groups]
                + [weight_block(*group) for group in groups],
                [grid_block((count * unit, cols)) for _, count in groups],
                [jax.ShapeDtypeStruct((count * unit, features), jnp.bfloat16) for _, count in groups],
                "update",
                12,
            ),
            place,
            grad_own,
            grad_other,
            *[hidden] * (2 * total),
            *[weights] * total,
        )

    def begin(blocks):
        def body(p, c, h, *refs):
            *w, o = refs
            o[...] = sum(
                mm(h[0, 0, :, at * unit : (at + count) * unit], block[...])
                for (at, count), block in zip(GROUPS, w)
            )

        return run(
            call(
                body,
                (4,),
                [pl.BlockSpec((1, 1, tokens, ff), lambda n, p, c: (0, 1, 0, 0))]
                + [grid_block((count * unit, cols)) for _, count in GROUPS[:-1]],
                grid_block((tokens, cols)),
                jax.ShapeDtypeStruct((tokens, features), jnp.float32),
                "begin",
                20,
            ),
            place,
            hidden,
            *blocks,
        )

    def finish(begun, block):
        def body(p, c, a, h, w, *refs):
            *outs, acc = refs
            acc[...] = FACTOR * (a[...] + mm(h[0, 0], w[...]))
            for (left, right), o in zip(((1, 3), (1, 2), (0, 3), (0, 2)), outs):
                at = pl.multiple_of(p[left] * half + p[right] * quarter, quarter)
                o[...] = acc[pl.ds(at, quarter), :].astype(o.dtype)

        kinds = (jnp.bfloat16, jnp.bfloat16, jnp.float32, jnp.float32)
        return run(
            call(
                body,
                (4,),
                [
                    grid_block((tokens, cols)),
                    pl.BlockSpec((1, 1, tokens, 2 * unit), lambda n, p, c: (0, 1, 0, UNITS // 2 - 1)),
                    grid_block((2 * unit, cols)),
                ],
                [grid_block((quarter, cols))] * 4,
                [jax.ShapeDtypeStruct((quarter, features), kind) for kind in kinds],
                "finish",
                10,
                scratch=[pltpu.VMEM((tokens, cols), jnp.float32)],
            ),
            place,
            begun,
            hidden,
            block,
        )

    def gather_rows(p, scale, quarters, rows_of):
        spots = ((0, 2), (0, 3), (1, 2), (1, 3))
        for (left, right), q in zip(spots, quarters):
            at = pl.multiple_of(p[left] * half + p[right] * quarter, quarter)
            rows_of[pl.ds(at, quarter), :] = q[...] * scale

    def output_own(grads, own, got):
        def body(p, c, h, q0, q1, q2, q3, *refs):
            *refs, o, g = refs
            gather_rows(p, c[0].astype(jnp.bfloat16), (q0, q1, q2, q3), g)
            for i, (at, count) in enumerate(GROUPS):
                span = slice(at * unit, (at + count) * unit)
                base = c[0] * refs[i][...].astype(jnp.float32)
                if i < len(GROUPS) - 1:
                    base = base + c[1] * refs[len(GROUPS) + i][...].astype(jnp.float32)
                grad = mm_rows(h[0, 0, :, span], g[...])
                o[0, span, :] = (base - LEARN_RATE * FACTOR * grad).astype(o.dtype)

        blocks = [grid_block((count * unit, cols)) for _, count in GROUPS]
        return run(
            call(
                body,
                (4,),
                [pl.BlockSpec((1, 1, tokens, ff), lambda n, p, c: (0, 1, 0, 0))]
                + [grid_block((quarter, cols))] * 4
                + blocks
                + blocks[:-1],
                pl.BlockSpec((1, ff, cols), lambda n, p, c: (0, 0, n)),
                jax.ShapeDtypeStruct(weights.shape, weights.dtype),
                "output_own",
                28,
                scratch=[pltpu.VMEM((tokens, cols), jnp.bfloat16)],
            ),
            coef,
            hidden,
            *grads,
            *own,
            *got,
        )

    def output_far(grads, base, x_top, x_low):
        def body(p, c, ha, hb, q0, q1, q2, q3, b, xt, xl, o, g):
            gather_rows(p, c[1].astype(jnp.bfloat16), (q0, q1, q2, q3), g)
            for at, count in GROUPS:
                span = slice(at * unit, (at + count) * unit)
                first = at * unit - edge
                h = ha[:, span] if first < 0 else hb[:, first : first + count * unit]
                total = b[0, span, :].astype(jnp.float32) - LEARN_RATE * FACTOR * mm_rows(h, g[...])
                if at == UNITS - 2:
                    rest = jnp.concatenate([xt[...], xl[...]], axis=0)
                    total = total + c[1] * rest.astype(jnp.float32)
                o[0, span, :] = total.astype(o.dtype)

        whole = pl.BlockSpec((1, ff, narrow), lambda n, p, c: (0, 0, n))
        return run(
            call(
                body,
                (8,),
                [
                    pl.BlockSpec((tokens, edge), lambda n, p, c: (0, 0)),
                    pl.BlockSpec((tokens, ff - edge), lambda n, p, c: (0, 0)),
                ]
                + [grid_block((quarter, narrow))] * 4
                + [whole] + [grid_block((unit, narrow))] * 2,
                whole,
                jax.ShapeDtypeStruct(weights.shape, weights.dtype),
                "output_far",
                14,
                scratch=[pltpu.VMEM((tokens, narrow), jnp.bfloat16)],
            ),
            coef,
            *borrowed,
            *grads,
            base,
            x_top,
            x_low,
        )

    def mix(scale_a, a, scale_b, b):
        return (scale_a * a.astype(jnp.float32) + scale_b * b.astype(jnp.float32)).astype(jnp.bfloat16)

    def add(kept, *parts):
        return sum([part.astype(jnp.float32) for part in parts], kept).astype(jnp.bfloat16)

    sent, kept = forward()
    sent, raw_hidden, late = meet(sent, raw_hidden, stragglers)
    summed = add(kept, permute(sent, 0, 1))
    early_part, late_part = raw_hidden[0, 1, :, :edge], raw_hidden[0, 1, :, edge:]
    from_z = permute(summed, 0, 2)
    borrowed = [permute(early_part, 2, 0)]
    turn[0], borrowed[0] = meet(turn[0], borrowed[0])

    def pair(step, low, high):
        count = lax.dynamic_index_in_dim(late[step], low, keepdims=False)
        count += lax.dynamic_index_in_dim(late[step], high, keepdims=False)
        return jnp.where(count == 0, jnp.float32(0.5), jnp.float32(0.0))

    near, mine = pair(0, replica, replica ^ 1), pair(1, replica, replica ^ 2)
    coef = jnp.stack([1 - mine, mine])
    from_z, near, coef, late_part = meet(from_z, near, coef, late_part)
    borrowed.append(permute(late_part, 2, 0))

    grad_own = norm_backward(0, summed, from_z)
    grad_other = permute(grad_own, 0, 1)

    updated = update(GROUPS[:1], grad_own, grad_other)
    updated += update(GROUPS[1:], grad_own, grad_other)
    got = []
    for i in range(len(GROUPS)):
        if i > 1:
            updated[i], got[i - 2] = meet(updated[i], got[i - 2])
        got.append(permute(updated[i], 1, 0))
    averaged, x_got = [], []
    for i in range(len(GROUPS)):
        if i > 1:
            got[i], x_got[i - 2] = meet(got[i], x_got[i - 2])
        elif i == 0:
            got[i], borrowed[1] = meet(got[i], borrowed[1])
        if i == len(GROUPS) - 1:
            begun = begin(averaged)
            got[i], begun = meet(got[i], begun)
        averaged.append(mix(1 - near, updated[i], near, got[i]))
        if i < len(GROUPS) - 1:
            x_got.append(permute(averaged[i], 2, 0))

    sent_out, sent_stay, kept_out, kept_stay = finish(begun, averaged[-1])
    outgoing = add(kept_out, permute(sent_out, 0, 1))
    outgoing, x_got[-1] = meet(outgoing, x_got[-1])
    incoming = permute(outgoing, 0, 2)
    x_top = permute(averaged[-1][:unit], 2, 0)
    incoming, x_top = meet(incoming, x_top)
    staying = kept_stay + permute(sent_stay, 0, 1).astype(jnp.float32)
    mine_q = norm_backward(1, staying, incoming)
    final, mine_q = meet(averaged[-1][unit:], mine_q)
    near_q = permute(mine_q, 0, 2)
    far_q = permute(mine_q, 2, 0)
    near_q, far_q = meet(near_q, far_q)
    far_near = permute(far_q, 0, 2)
    x_low = permute(final, 2, 0)
    base = output_own((mine_q, near_q, permute(mine_q, 0, 1), permute(near_q, 0, 1)), averaged, x_got)
    far_near, base = meet(far_near, base)
    return output_far((far_q, far_near, permute(far_q, 0, 1), permute(far_near, 0, 1)), base, x_top, x_low)


def solution(mesh):
    placed = (
        P("replica", "tensor", None),
        P("replica", None, None, "tensor"),
        P("replica", None, None, None),
        P(),
        P(),
    )
    return jax.shard_map(
        on_device,
        mesh=mesh,
        in_specs=placed,
        out_specs=P("replica", "tensor", None),
        check_vma=False,
    )
```

time: 288 us -> 273 us (0.948)
  waiting for transfers between devices: 176 us -> 163 us
  Pallas kernels: 59.3 us -> 53.3 us
    ppermute x27 -> x30, waiting for transfers between devices: 176 us -> 163 us  [permute(): return lax.ppermute(block, ('replica', 'tensor'), route)]
    pallas_call x11 -> x9, Pallas kernels: 59.3 us -> 53.3 us  [run(): out = kernel(turn[0], *args)]
    squeeze x1 -> x2, local copies, waits for them, and re-layouts: 1.35 us -> 4.33 us  [the longest x1 2.26 us: on_device(): raw_hidden[0, 1, :, :edge]]
    ppermute x27 -> x30, starting transfers between devices: 40.9 us -> 42.1 us  [permute(): return lax.ppermute(block, ('replica', 'tensor'), route)]
  transfers between devices with their start and end apart: 27 -> 30, of which waited for: 18 -> 19; matrix products, arithmetic and copies ran while one was open for 3% -> 4% of each run, Pallas kernels for 14% -> 10%
where the time goes in v2:
time: 273 us; the launch traced here: 272 us
  waiting for transfers between devices  163 us (60%)
  Pallas kernels  53.3 us (20%)
  starting transfers between devices  42.1 us (15%)
  local copies, waits for them, and re-layouts  6.04 us (2%)
  other arithmetic  4.97 us (2%)
    ppermute x30, waiting for transfers between devices, permute(): return lax.ppermute(block, ('replica', 'tensor'), route)  163 us
    pallas_call x9, Pallas kernels, run(): out = kernel(turn[0], *args)  53.3 us
    ppermute x30, starting transfers between devices, permute(): return lax.ppermute(block, ('replica', 'tensor'), route)  42.1 us
  transfers between devices with their start and end apart: 30, of which 19 were waited for; matrix products, arithmetic and copies ran while one was open for 4% of the time, Pallas kernels for 10%

profile of v2, /device:TPU:1, one launch (start us, length us, event | category | flops | bytes accessed | tf_op | source)
XLA Modules:
  0.0 272.4 jit_solution(164478603667362769)
XLA Ops:
  0.1 8.3 %forward.1 = (bf16[256,2048]{1,0:T(8,128)(2,1)S(1)}, f32[256,2048]{1,0:T(8,128)S(1)}) custom-call(s32[4]{0:T(128)S(1)} %pad_add_fusion.p.c, s32[4]{0:T(128)S(1)} %pad_add_fusion.p.c, bf16[1,2,512,1792]{3,2,1,0:T(8,128)(2,1)} %h.7, bf16[1,1792,2048]{2,1,0:T(8,128)(2,1)} %refs_19_.1, bf16[1,1792,2048]{2,1,0:T(8,128)(2,1)} %refs_19_.1), custom_call_target="tpu_custom_call" | custom-call | flops 1 | bytes 1 | tf_op jit(solution)/shard_map/forward/pallas_call | solution.py:75
  20.7 16.4 %collective-permute-done.ha = bf16[512,1024]{1,0:T(8,128)(2,1)S(1)} collective-permute-done((bf16[512,1024]{1,0:T(8,128)(2,1)}, bf16[512,1024]{1,0:T(8,128)(2,1)S(1)}, u32[]{:S(2)}, u32[]{:S(2)}) %collective-permute-start) | collective-permute-done | bytes 1048608 | tf_op jit(solution)/shard_map/ppermute | solution.py:72
  38.7 2.8 %norm_backward.2.refs_0_ = bf16[256,2048]{1,0:T(8,128)(2,1)S(1)} custom-call(s32[4]{0:T(128)S(1)} %pad_add_fusion.p.c, s32[4]{0:T(128)S(1)} %pad_add_fusion.p.c, bf16[256,2048]{1,0:T(8,128)(2,1)S(1)} %add_convert_fusion.7.s, bf16[256,2048]{1,0:T(8,128)(2,1)S(1)} %collective-permute-done.2.r, bf16[1,2,512,2048]{3,2,1,0:T(8,128)(2,1)} %t.3, f32[1,2048]{1,0:T(1,128)S(1)} %bitcast.12), custom_call_target="tpu_custom_call" | custom-call | flops 1 | bytes 1 | tf_op jit(solution)/shard_map/norm_backward/pallas_call | solution.py:75
  44.8 3.9 %update.2 = bf16[256,2048]{1,0:T(8,128)(2,1)S(1)} custom-call(s32[4]{0:T(128)S(1)} %pad_add_fusion.p.c, s32[4]{0:T(128)S(1)} %pad_add_fusion.p.c, bf16[256,2048]{1,0:T(8,128)(2,1)S(1)} %norm_backward.2.refs_0_, bf16[256,2048]{1,0:T(8,128)(2,1)S(1)} %collective-permute-done.3.refs_1_, bf16[1,2,512,1792]{3,2,1,0:T(8,128)(2,1)} %h.7, ...), custom_call_target="tpu_custom_call" | custom-call | flops 1 | bytes 1 | tf_op jit(solution)/shard_map/update/pallas_call | solution.py:75
  48.7 3.5 %collective-permute-start.4 = (bf16[256,2048]{1,0:T(8,128)(2,1)S(1)}, bf16[256,2048]{1,0:T(8,128)(2,1)}, u32[]{:S(2)}, u32[]{:S(2)}) collective-permute-start(bf16[256,2048]{1,0:T(8,128)(2,1)S(1)} %update.2), channel_id=1, source_target_pairs={{0,4},{1,5},{2,6},{3,7},{4,0},{5,1},{6,2},{7,3},{8,12},{9,13},{10,... | collective-permute-start | bytes 3145736 | tf_op jit(solution)/shard_map/ppermute | solution.py:72
  52.9 7.9 %update.3 = (bf16[256,2048]{1,0:T(8,128)(2,1)S(1)}, bf16[256,2048]{1,0:T(8,128)(2,1)S(1)}, bf16[256,2048]{1,0:T(8,128)(2,1)S(1)}, bf16[256,2048]{1,0:T(8,128)(2,...) custom-call(s32[4]{0:T(128)S(1)} %pad_add_fusion.p.c, s32[4]{0:T(128)S(1)} %pad_add_fusion.p.c, ...), custom_call_target="tpu_custom_call" | custom-call | flops 1 | bytes 1 | tf_op jit(solution)/shard_map/update/pallas_call | solution.py:75
  61.0 14.5 %collective-permute-done.4 = bf16[256,2048]{1,0:T(8,128)(2,1)} collective-permute-done((bf16[256,2048]{1,0:T(8,128)(2,1)S(1)}, bf16[256,2048]{1,0:T(8,128)(2,1)}, u32[]{:S(2)}, u32[]{:S(2)}) %collective-permute-start.4) | collective-permute-done | bytes 1048608 | tf_op jit(solution)/shard_map/ppermute | solution.py:72
  75.5 2.6 collective-permute-start.7
  80.6 17.2 %collective-permute-done.6 = bf16[256,2048]{1,0:T(8,128)(2,1)S(1)} collective-permute-done((bf16[256,2048]{1,0:T(8,128)(2,1)S(1)}, bf16[256,2048]{1,0:T(8,128)(2,1)S(1)}, u32[]{:S(2)}, u32[]{:S(2)}) %collective-permute-start.6) | collective-permute-done | bytes 1048608 | tf_op jit(solution)/shard_map/ppermute | solution.py:72
  97.9 2.6 collective-permute-start.9
  101.8 18.5 %collective-permute-done.7 = bf16[256,2048]{1,0:T(8,128)(2,1)S(1)} collective-permute-done((bf16[256,2048]{1,0:T(8,128)(2,1)S(1)}, bf16[256,2048]{1,0:T(8,128)(2,1)S(1)}, u32[]{:S(2)}, u32[]{:S(2)}) %collective-permute-start.7) | collective-permute-done | bytes 1048608 | tf_op jit(solution)/shard_map/ppermute | solution.py:72
  120.3 2.6 collective-permute-start.11
  124.3 18.5 %collective-permute-done.9 = bf16[256,2048]{1,0:T(8,128)(2,1)S(1)} collective-permute-done((bf16[256,2048]{1,0:T(8,128)(2,1)S(1)}, bf16[256,2048]{1,0:T(8,128)(2,1)S(1)}, u32[]{:S(2)}, u32[]{:S(2)}) %collective-permute-start.9) | collective-permute-done | bytes 1048608 | tf_op jit(solution)/shard_map/ppermute | solution.py:72
  146.8 18.5 %collective-permute-done.11 = bf16[256,2048]{1,0:T(8,128)(2,1)S(1)} collective-permute-done((bf16[256,2048]{1,0:T(8,128)(2,1)S(1)}, bf16[256,2048]{1,0:T(8,128)(2,1)S(1)}, u32[]{:S(2)}, u32[]{:S(2)}) %collective-permute-start.11) | collective-permute-done | bytes 1048608 | tf_op jit(solution)/shard_map/ppermute | solution.py:72
  166.6 2.6 collective-permute-start.15
  170.9 16.9 %collective-permute-done.13 = bf16[256,2048]{1,0:T(8,128)(2,1)S(1)} collective-permute-done((bf16[256,2048]{1,0:T(8,128)(2,1)S(1)}, bf16[256,2048]{1,0:T(8,128)(2,1)S(1)}, u32[]{:S(2)}, u32[]{:S(2)}) %collective-permute-start.13) | collective-permute-done | bytes 1048608 | tf_op jit(solution)/shard_map/ppermute | solution.py:72
  189.2 6.6 %begin.1.a = f32[512,2048]{1,0:T(8,128)S(1)} custom-call(s32[4]{0:T(128)S(1)} %pad_add_fusion.p.c, s32[4]{0:T(128)S(1)} %pad_add_fusion.p.c, bf16[1,2,512,1792]{3,2,1,0:T(8,128)(2,1)} %h.7, bf16[256,2048]{1,0:T(8,128)(2,1)S(1)} %add_convert_fusion.6.refs_0_, bf16[256,2048]{1,0:T(8,128)(2,1)S(1)} %add_convert_fusion.5.refs_1_, ...), custom_call_target="tpu_custom_call" | custom-call | flops 1 | bytes 1 | tf_op jit(solution)/shard_map/begin/pallas_call | solution.py:75
  195.8 14.4 %collective-permute-done.15 = bf16[256,2048]{1,0:T(8,128)(2,1)S(1)} collective-permute-done((bf16[256,2048]{1,0:T(8,128)(2,1)S(1)}, bf16[256,2048]{1,0:T(8,128)(2,1)S(1)}, u32[]{:S(2)}, u32[]{:S(2)}) %collective-permute-start.15) | collective-permute-done | bytes 1048608 | tf_op jit(solution)/shard_map/ppermute | solution.py:72
  210.7 3.5 %finish.1 = (bf16[128,2048]{1,0:T(8,128)(2,1)S(1)}, bf16[128,2048]{1,0:T(8,128)(2,1)S(1)}, f32[128,2048]{1,0:T(8,128)S(1)}, f32[128,2048]{1,0:T(8,128)S(1)}) custom-call(s32[4]{0:T(128)S(1)} %pad_add_fusion.p.c, s32[4]{0:T(128)S(1)} %pad_add_fusion.p.c, f32[512,2048]{1,0:T(8,128)S(1)} %begin.1.a, bf16[1,2,512,1792]{3,2,1,0:T(8,128)(2,1)} %h.7, ...), custom_call_target="tpu_custom_call" | custom-call | flops 1 | bytes 1 | tf_op jit(solution)/shard_map/finish/pallas_call | solution.py:75
  218.0 10.5 %collective-permute-done.21.xt = bf16[128,2048]{1,0:T(8,128)(2,1)S(1)} collective-permute-done((bf16[128,2048]{1,0:T(8,128)(2,1)S(1)}, bf16[128,2048]{1,0:T(8,128)(2,1)S(1)}, u32[]{:S(2)}, u32[]{:S(2)}) %collective-permute-start.21) | collective-permute-done | bytes 524320 | tf_op jit(solution)/shard_map/ppermute | solution.py:72
  235.8 7.4 %collective-permute-done.23.q0 = bf16[128,2048]{1,0:T(8,128)(2,1)S(1)} collective-permute-done((bf16[128,2048]{1,0:T(8,128)(2,1)S(1)}, bf16[128,2048]{1,0:T(8,128)(2,1)S(1)}, u32[]{:S(2)}, u32[]{:S(2)}) %collective-permute-start.23) | collective-permute-done | bytes 524320 | tf_op jit(solution)/shard_map/ppermute | solution.py:72
  243.7 3.0 %collective-permute-start.25 = (bf16[128,2048]{1,0:T(8,128)(2,1)S(1)}, bf16[128,2048]{1,0:T(8,128)(2,1)S(1)}, u32[]{:S(2)}, u32[]{:S(2)}) collective-permute-start(bf16[128,2048]{1,0:T(8,128)(2,1)S(1)} %collective-permute-done.22.q1), channel_id=1, source_target_pairs={{0,1},{1,0},{2,3},{3,2},{4,5},{5,4},{6,7},{7,6},{8,9},{9,8},{10,11... | collective-permute-start | bytes 1572872 | tf_op jit(solution)/shard_map/ppermute | solution.py:72
  249.4 8.4 %output_own.1.b = bf16[1,1792,2048]{2,1,0:T(8,128)(2,1)S(1)} custom-call(s32[4]{0:T(128)S(1)} %pad_add_fusion.p.c, f32[2]{0:T(128)S(1)} %pad_maximum_fusion.c, bf16[1,2,512,1792]{3,2,1,0:T(8,128)(2,1)} %h.7, bf16[128,2048]{1,0:T(8,128)(2,1)S(1)} %norm_backward.3.q0, bf16[128,2048]{1,0:T(8,128)(2,1)S(1)} %collective-permute-done.22.q1, ...), custom_call_target="tpu_custom_call" | custom-call | flops 1 | bytes 1 | tf_op jit(solution)/shard_map/output_own/pallas_call | solution.py:75
  262.6 9.8 %output_far.1 = bf16[1,1792,2048]{2,1,0:T(8,128)(2,1)} custom-call(s32[4]{0:T(128)S(1)} %pad_add_fusion.p.c, f32[2]{0:T(128)S(1)} %pad_maximum_fusion.c, bf16[512,1024]{1,0:T(8,128)(2,1)S(1)} %copy-done.1, bf16[512,768]{1,0:T(8,128)(2,1)} %collective-permute-done.5.hb, bf16[128,2048]{1,0:T(8,128)(2,1)S(1)} %collective-permute-done.23.q0, ...), custom_call_target="tpu_custom_call" | custom-call | flops 1 | bytes 1 | tf_op jit(solution)/shard_map/output_far/pallas_call | solution.py:75
  (70 shorter events, 48.7 us)
Async XLA Ops:
  12.1 25.0 %collective-permute-start = (bf16[512,1024]{1,0:T(8,128)(2,1)}, bf16[512,1024]{1,0:T(8,128)(2,1)S(1)}, u32[]{:S(2)}, u32[]{:S(2)}) collective-permute-start(bf16[512,1024]{1,0:T(8,128)(2,1)} %slice_bitcast_fusion), channel_id=1, source_target_pairs={{0,8},{1,9},{2,10},{3,11},{4,12},{5,13},{6,14},{7,15},{8,0},{9,1},... | collective-permute-start | bytes 3145736 | tf_op jit(solution)/shard_map/ppermute | solution.py:72
  13.7 24.9 %collective-permute-start.2 = (bf16[256,2048]{1,0:T(8,128)(2,1)S(1)}, bf16[256,2048]{1,0:T(8,128)(2,1)S(1)}, u32[]{:S(2)}, u32[]{:S(2)}) collective-permute-start(bf16[256,2048]{1,0:T(8,128)(2,1)S(1)} %add_convert_fusion.7.s), channel_id=1, source_target_pairs={{0,2},{1,3},{2,0},{3,1},{4,6},{5,7},{6,4},{7,5},{8,10},{9,11},{10,... | collective-permute-start | bytes 3145736 | tf_op jit(solution)/shard_map/ppermute | solution.py:72
  48.7 26.8 %collective-permute-start.4 = (bf16[256,2048]{1,0:T(8,128)(2,1)S(1)}, bf16[256,2048]{1,0:T(8,128)(2,1)}, u32[]{:S(2)}, u32[]{:S(2)}) collective-permute-start(bf16[256,2048]{1,0:T(8,128)(2,1)S(1)} %update.2), channel_id=1, source_target_pairs={{0,4},{1,5},{2,6},{3,7},{4,0},{5,1},{6,2},{7,3},{8,12},{9,13},{10,... | collective-permute-start | bytes 3145736 | tf_op jit(solution)/shard_map/ppermute | solution.py:72
  52.2 23.3 %collective-permute-start.5 = (bf16[512,768]{1,0:T(8,128)(2,1)}, bf16[512,768]{1,0:T(8,128)(2,1)}, u32[]{:S(2)}, u32[]{:S(2)}) collective-permute-start(bf16[512,768]{1,0:T(8,128)(2,1)} %slice_bitcast_fusion.1), channel_id=1, source_target_pairs={{0,8},{1,9},{2,10},{3,11},{4,12},{5,13},{6,14},{7,15},{8,0},{9,1},... | collective-permute-start | bytes 2359304 | tf_op jit(solution)/shard_map/ppermute | solution.py:72
  60.9 37.0 %collective-permute-start.6 = (bf16[256,2048]{1,0:T(8,128)(2,1)S(1)}, bf16[256,2048]{1,0:T(8,128)(2,1)S(1)}, u32[]{:S(2)}, u32[]{:S(2)}) collective-permute-start(bf16[256,2048]{1,0:T(8,128)(2,1)S(1)} %get-tuple-element.112), channel_id=1, source_target_pairs={{0,4},{1,5},{2,6},{3,7},{4,0},{5,1},{6,2},{7,3},{8,12},{9,13},{10,... | collective-permute-start | bytes 3145736 | tf_op jit(solution)/shard_map/ppermute | solution.py:72
  75.5 44.8 %collective-permute-start.7 = (bf16[256,2048]{1,0:T(8,128)(2,1)S(1)}, bf16[256,2048]{1,0:T(8,128)(2,1)S(1)}, u32[]{:S(2)}, u32[]{:S(2)}) collective-permute-start(bf16[256,2048]{1,0:T(8,128)(2,1)S(1)} %get-tuple-element.115), channel_id=1, source_target_pairs={{0,4},{1,5},{2,6},{3,7},{4,0},{5,1},{6,2},{7,3},{8,12},{9,13},{10,... | collective-permute-start | bytes 3145736 | tf_op jit(solution)/shard_map/ppermute | solution.py:72
  79.8 40.6 %collective-permute-start.8 = (bf16[256,2048]{1,0:T(8,128)(2,1)S(1)}, bf16[256,2048]{1,0:T(8,128)(2,1)S(1)}, u32[]{:S(2)}, u32[]{:S(2)}) collective-permute-start(bf16[256,2048]{1,0:T(8,128)(2,1)S(1)} %add_convert_fusion.6.refs_0_), channel_id=1, source_target_pairs={{0,8},{1,9},{2,10},{3,11},{4,12},{5,13},{6,14},{7,15},{8,0},{9,1},... | collective-permute-start | bytes 3145736 | tf_op jit(solution)/shard_map/ppermute | solution.py:72
  97.9 44.9 %collective-permute-start.9 = (bf16[256,2048]{1,0:T(8,128)(2,1)S(1)}, bf16[256,2048]{1,0:T(8,128)(2,1)S(1)}, u32[]{:S(2)}, u32[]{:S(2)}) collective-permute-start(bf16[256,2048]{1,0:T(8,128)(2,1)S(1)} %get-tuple-element.119), channel_id=1, source_target_pairs={{0,4},{1,5},{2,6},{3,7},{4,0},{5,1},{6,2},{7,3},{8,12},{9,13},{10,... | collective-permute-start | bytes 3145736 | tf_op jit(solution)/shard_map/ppermute | solution.py:72
  101.0 41.8 %collective-permute-start.10 = (bf16[256,2048]{1,0:T(8,128)(2,1)S(1)}, bf16[256,2048]{1,0:T(8,128)(2,1)S(1)}, u32[]{:S(2)}, u32[]{:S(2)}) collective-permute-start(bf16[256,2048]{1,0:T(8,128)(2,1)S(1)} %add_convert_fusion.5.refs_1_), channel_id=1, source_target_pairs={{0,8},{1,9},{2,10},{3,11},{4,12},{5,13},{6,14},{7,15},{8,0},{9,1},... | collective-permute-start | bytes 3145736 | tf_op jit(solution)/shard_map/ppermute | solution.py:72
  120.3 44.9 %collective-permute-start.11 = (bf16[256,2048]{1,0:T(8,128)(2,1)S(1)}, bf16[256,2048]{1,0:T(8,128)(2,1)S(1)}, u32[]{:S(2)}, u32[]{:S(2)}) collective-permute-start(bf16[256,2048]{1,0:T(8,128)(2,1)S(1)} %get-tuple-element.123), channel_id=1, source_target_pairs={{0,4},{1,5},{2,6},{3,7},{4,0},{5,1},{6,2},{7,3},{8,12},{9,13},{10,... | collective-permute-start | bytes 3145736 | tf_op jit(solution)/shard_map/ppermute | solution.py:72
  123.4 41.8 %collective-permute-start.12 = (bf16[256,2048]{1,0:T(8,128)(2,1)S(1)}, bf16[256,2048]{1,0:T(8,128)(2,1)S(1)}, u32[]{:S(2)}, u32[]{:S(2)}) collective-permute-start(bf16[256,2048]{1,0:T(8,128)(2,1)S(1)} %add_convert_fusion.4.refs_2_), channel_id=1, source_target_pairs={{0,8},{1,9},{2,10},{3,11},{4,12},{5,13},{6,14},{7,15},{8,0},{9,1},... | collective-permute-start | bytes 3145736 | tf_op jit(solution)/shard_map/ppermute | solution.py:72
  143.3 27.6 %collective-permute-start.14 = (bf16[256,2048]{1,0:T(8,128)(2,1)S(1)}, bf16[256,2048]{1,0:T(8,128)(2,1)S(1)}, u32[]{:S(2)}, u32[]{:S(2)}) collective-permute-start(bf16[256,2048]{1,0:T(8,128)(2,1)S(1)} %add_convert_fusion.3.refs_3_), channel_id=1, source_target_pairs={{0,8},{1,9},{2,10},{3,11},{4,12},{5,13},{6,14},{7,15},{8,0},{9,1},... | collective-permute-start | bytes 3145736 | tf_op jit(solution)/shard_map/ppermute | solution.py:72
  144.1 43.6 %collective-permute-start.13 = (bf16[256,2048]{1,0:T(8,128)(2,1)S(1)}, bf16[256,2048]{1,0:T(8,128)(2,1)S(1)}, u32[]{:S(2)}, u32[]{:S(2)}) collective-permute-start(bf16[256,2048]{1,0:T(8,128)(2,1)S(1)} %get-tuple-element.127), channel_id=1, source_target_pairs={{0,4},{1,5},{2,6},{3,7},{4,0},{5,1},{6,2},{7,3},{8,12},{9,13},{10,... | collective-permute-start | bytes 3145736 | tf_op jit(solution)/shard_map/ppermute | solution.py:72
  165.7 30.1 %collective-permute-start.16 = (bf16[256,2048]{1,0:T(8,128)(2,1)S(1)}, bf16[256,2048]{1,0:T(8,128)(2,1)S(1)}, u32[]{:S(2)}, u32[]{:S(2)}) collective-permute-start(bf16[256,2048]{1,0:T(8,128)(2,1)S(1)} %add_convert_fusion.2.refs_4_), channel_id=1, source_target_pairs={{0,8},{1,9},{2,10},{3,11},{4,12},{5,13},{6,14},{7,15},{8,0},{9,1},... | collective-permute-start | bytes 3145736 | tf_op jit(solution)/shard_map/ppermute | solution.py:72
  166.6 43.6 %collective-permute-start.15 = (bf16[256,2048]{1,0:T(8,128)(2,1)S(1)}, bf16[256,2048]{1,0:T(8,128)(2,1)S(1)}, u32[]{:S(2)}, u32[]{:S(2)}) collective-permute-start(bf16[256,2048]{1,0:T(8,128)(2,1)S(1)} %get-tuple-element.130), channel_id=1, source_target_pairs={{0,4},{1,5},{2,6},{3,7},{4,0},{5,1},{6,2},{7,3},{8,12},{9,13},{10,... | collective-permute-start | bytes 3145736 | tf_op jit(solution)/shard_map/ppermute | solution.py:72
  188.1 28.6 %collective-permute-start.19 = (bf16[256,2048]{1,0:T(8,128)(2,1)S(1)}, bf16[256,2048]{1,0:T(8,128)(2,1)S(1)}, u32[]{:S(2)}, u32[]{:S(2)}) collective-permute-start(bf16[256,2048]{1,0:T(8,128)(2,1)S(1)} %add_convert_fusion.1.refs_5_), channel_id=1, source_target_pairs={{0,8},{1,9},{2,10},{3,11},{4,12},{5,13},{6,14},{7,15},{8,0},{9,1},... | collective-permute-start | bytes 3145736 | tf_op jit(solution)/shard_map/ppermute | solution.py:72
  215.3 13.2 %collective-permute-start.21 = (bf16[128,2048]{1,0:T(8,128)(2,1)S(1)}, bf16[128,2048]{1,0:T(8,128)(2,1)S(1)}, u32[]{:S(2)}, u32[]{:S(2)}) collective-permute-start(bf16[128,2048]{1,0:T(8,128)(2,1)S(1)} %get-tuple-element.168), channel_id=1, source_target_pairs={{0,8},{1,9},{2,10},{3,11},{4,12},{5,13},{6,14},{7,15},{8,0},{9,1},... | collective-permute-start | bytes 1572872 | tf_op jit(solution)/shard_map/ppermute | solution.py:72
  216.8 12.6 %collective-permute-start.20 = (bf16[128,2048]{1,0:T(8,128)(2,1)S(1)}, bf16[128,2048]{1,0:T(8,128)(2,1)S(1)}, u32[]{:S(2)}, u32[]{:S(2)}) collective-permute-start(bf16[128,2048]{1,0:T(8,128)(2,1)S(1)} %add_convert_fusion.8), channel_id=1, source_target_pairs={{0,2},{1,3},{2,0},{3,1},{4,6},{5,7},{6,4},{7,5},{8,10},{9,11},{10,... | collective-permute-start | bytes 1572872 | tf_op jit(solution)/shard_map/ppermute | solution.py:72
  231.6 11.7 %collective-permute-start.23 = (bf16[128,2048]{1,0:T(8,128)(2,1)S(1)}, bf16[128,2048]{1,0:T(8,128)(2,1)S(1)}, u32[]{:S(2)}, u32[]{:S(2)}) collective-permute-start(bf16[128,2048]{1,0:T(8,128)(2,1)S(1)} %norm_backward.3.q0), channel_id=1, source_target_pairs={{0,8},{1,9},{2,10},{3,11},{4,12},{5,13},{6,14},{7,15},{8,0},{9,1},... | collective-permute-start | bytes 1572872 | tf_op jit(solution)/shard_map/ppermute | solution.py:72
  232.4 11.3 %collective-permute-start.22 = (bf16[128,2048]{1,0:T(8,128)(2,1)S(1)}, bf16[128,2048]{1,0:T(8,128)(2,1)S(1)}, u32[]{:S(2)}, u32[]{:S(2)}) collective-permute-start(bf16[128,2048]{1,0:T(8,128)(2,1)S(1)} %norm_backward.3.q0), channel_id=1, source_target_pairs={{0,2},{1,3},{2,0},{3,1},{4,6},{5,7},{6,4},{7,5},{8,10},{9,11},{10,... | collective-permute-start | bytes 1572872 | tf_op jit(solution)/shard_map/ppermute | solution.py:72
  233.8 15.6 %collective-permute-start.24 = (bf16[128,2048]{1,0:T(8,128)(2,1)S(1)}, bf16[128,2048]{1,0:T(8,128)(2,1)S(1)}, u32[]{:S(2)}, u32[]{:S(2)}) collective-permute-start(bf16[128,2048]{1,0:T(8,128)(2,1)S(1)} %norm_backward.3.q0), channel_id=1, source_target_pairs={{0,1},{1,0},{2,3},{3,2},{4,5},{5,4},{6,7},{7,6},{8,9},{9,8},{10,11... | collective-permute-start | bytes 1572872 | tf_op jit(solution)/shard_map/ppermute | solution.py:72
  246.8 13.6 %collective-permute-start.26 = (bf16[128,2048]{1,0:T(8,128)(2,1)S(1)}, bf16[128,2048]{1,0:T(8,128)(2,1)S(1)}, u32[]{:S(2)}, u32[]{:S(2)}) collective-permute-start(bf16[128,2048]{1,0:T(8,128)(2,1)S(1)} %collective-permute-done.23.q0), channel_id=1, source_target_pairs={{0,2},{1,3},{2,0},{3,1},{4,6},{5,7},{6,4},{7,5},{8,10},{9,11},{10,... | collective-permute-start | bytes 1572872 | tf_op jit(solution)/shard_map/ppermute | solution.py:72
  248.1 13.2 %collective-permute-start.29 = (bf16[128,2048]{1,0:T(8,128)(2,1)S(1)}, bf16[128,2048]{1,0:T(8,128)(2,1)S(1)}, u32[]{:S(2)}, u32[]{:S(2)}) collective-permute-start(bf16[128,2048]{1,0:T(8,128)(2,1)S(1)} %get-tuple-element.165), channel_id=1, source_target_pairs={{0,8},{1,9},{2,10},{3,11},{4,12},{5,13},{6,14},{7,15},{8,0},{9,1},... | collective-permute-start | bytes 1572872 | tf_op jit(solution)/shard_map/ppermute | solution.py:72
  248.8 12.5 %collective-permute-start.27 = (bf16[128,2048]{1,0:T(8,128)(2,1)S(1)}, bf16[128,2048]{1,0:T(8,128)(2,1)S(1)}, u32[]{:S(2)}, u32[]{:S(2)}) collective-permute-start(bf16[128,2048]{1,0:T(8,128)(2,1)S(1)} %collective-permute-done.23.q0), channel_id=1, source_target_pairs={{0,1},{1,0},{2,3},{3,2},{4,5},{5,4},{6,7},{7,6},{8,9},{9,8},{10,11... | collective-permute-start | bytes 1572872 | tf_op jit(solution)/shard_map/ppermute | solution.py:72
  (10 other events, 83.5 us)

commit v3 on v2

--- a/solution.py
+++ b/solution.py
@@ -49,10 +49,9 @@
     features = weights.shape[2]
     half = tokens // 2
     cols = features // 4
-    narrow = features // 8
     unit = ff // UNITS
     deep = ff // 2
-    edge = 8 * unit
+    edge = 6 * unit
     replica = lax.axis_index("replica")
     core = lax.rem(lax.axis_index("tensor"), 2)
     near_z = lax.div(lax.axis_index("tensor"), 2)
@@ -154,6 +153,7 @@
 
     def update(groups, grad_own, grad_other):
         total = len(groups)
+        across = cols if total > 1 else 2 * cols
 
         def body(p, c, *refs):
             go, gx = refs[:2]
@@ -167,17 +167,17 @@
             return pl.BlockSpec((1, 1, half, count * unit), lambda n, p, c: (0, 0, p[side], at // count))
 
         def weight_block(at, count):
-            return pl.BlockSpec((1, count * unit, cols), lambda n, p, c: (0, at // count, n))
-
-        return run(
-            call(
-                body,
-                (4,),
-                [grid_block((half, cols))] * 2
+            return pl.BlockSpec((1, count * unit, across), lambda n, p, c: (0, at // count, n))
+
+        return run(
+            call(
+                body,
+                (features // across,),
+                [grid_block((half, across))] * 2
                 + [hidden_block(0, *group) for group in groups]
                 + [hidden_block(1, *group) for group in groups]
                 + [weight_block(*group) for group in groups],
-                [grid_block((count * unit, cols)) for _, count in groups],
+                [grid_block((count * unit, across)) for _, count in groups],
                 [jax.ShapeDtypeStruct((count * unit, features), jnp.bfloat16) for _, count in groups],
                 "update",
                 12,
@@ -284,34 +284,50 @@
         )
 
     def output_far(grads, base, x_top, x_low):
+        tall = 2 * unit
+        early = edge // tall
+        last = UNITS // 2 - 1
+
         def body(p, c, ha, hb, q0, q1, q2, q3, b, xt, xl, o, g):
-            gather_rows(p, c[1].astype(jnp.bfloat16), (q0, q1, q2, q3), g)
-            for at, count in GROUPS:
-                span = slice(at * unit, (at + count) * unit)
-                first = at * unit - edge
-                h = ha[:, span] if first < 0 else hb[:, first : first + count * unit]
-                total = b[0, span, :].astype(jnp.float32) - LEARN_RATE * FACTOR * mm_rows(h, g[...])
-                if at == UNITS - 2:
-                    rest = jnp.concatenate([xt[...], xl[...]], axis=0)
-                    total = total + c[1] * rest.astype(jnp.float32)
-                o[0, span, :] = total.astype(o.dtype)
-
-        whole = pl.BlockSpec((1, ff, narrow), lambda n, p, c: (0, 0, n))
-        return run(
-            call(
-                body,
-                (8,),
+            step = pl.program_id(0)
+
+            @pl.when(step == 0)
+            def _():
+                gather_rows(p, c[1].astype(jnp.bfloat16), (q0, q1, q2, q3), g)
+
+            def emit(h, extra):
+                for j in range(4):
+                    side = slice(j * cols, (j + 1) * cols)
+                    total = b[0, :, side].astype(jnp.float32)
+                    total = total - LEARN_RATE * FACTOR * mm_rows(h[...], g[:, side])
+                    if extra:
+                        rest = jnp.concatenate([xt[:, side], xl[:, side]], axis=0)
+                        total = total + c[1] * rest.astype(jnp.float32)
+                    o[0, :, side] = total.astype(o.dtype)
+
+            pl.when(step < early)(lambda: emit(ha, False))
+            pl.when((step >= early) & (step < last))(lambda: emit(hb, False))
+            pl.when(step == last)(lambda: emit(hb, True))
+
+        def fixed(height):
+            return pl.BlockSpec((height, features), lambda n, p, c: (0, 0))
+
+        block = pl.BlockSpec((1, tall, features), lambda n, p, c: (0, n, 0))
+        return run(
+            call(
+                body,
+                (UNITS // 2,),
                 [
-                    pl.BlockSpec((tokens, edge), lambda n, p, c: (0, 0)),
-                    pl.BlockSpec((tokens, ff - edge), lambda n, p, c: (0, 0)),
+                    pl.BlockSpec((tokens, tall), lambda n, p, c: (0, jnp.minimum(n, early - 1))),
+                    pl.BlockSpec((tokens, tall), lambda n, p, c: (0, jnp.maximum(n - early, 0))),
                 ]
-                + [grid_block((quarter, narrow))] * 4
-                + [whole] + [grid_block((unit, narrow))] * 2,
-                whole,
+                + [fixed(quarter)] * 4
+                + [block, fixed(unit), fixed(unit)],
+                block,
                 jax.ShapeDtypeStruct(weights.shape, weights.dtype),
                 "output_far",
-                14,
-                scratch=[pltpu.VMEM((tokens, narrow), jnp.bfloat16)],
+                18,
+                scratch=[pltpu.VMEM((tokens, features), jnp.bfloat16)],
             ),
             coef,
             *borrowed,
@@ -328,8 +344,8 @@
         return sum([part.astype(jnp.float32) for part in parts], kept).astype(jnp.bfloat16)
 
     sent, kept = forward()
-    sent, raw_hidden, late = meet(sent, raw_hidden, stragglers)
     summed = add(kept, permute(sent, 0, 1))
+    summed, raw_hidden, late = meet(summed, raw_hidden, stragglers)
     early_part, late_part = raw_hidden[0, 1, :, :edge], raw_hidden[0, 1, :, edge:]
     from_z = permute(summed, 0, 2)
     borrowed = [permute(early_part, 2, 0)]

time: 273 us -> 271 us (level)
  waiting for transfers between devices: 163 us -> 160 us
    ppermute x30, waiting for transfers between devices: 163 us -> 160 us  [permute(): return lax.ppermute(block, ('replica', 'tensor'), route)]
  transfers between devices with their start and end apart: 30 -> 30, of which waited for: 19 -> 21; matrix products, arithmetic and copies ran while one was open for 4% -> 4% of each run, Pallas kernels for 10% -> 10%
where the time goes in v3:
time: 271 us; the launch traced here: 270 us
  waiting for transfers between devices  160 us (59%)
  Pallas kernels  51.6 us (19%)
  starting transfers between devices  44.6 us (16%)
  local copies, waits for them, and re-layouts  5.98 us (2%)
  other arithmetic  4.94 us (2%)
  between operations  2.77 us (1%)
    ppermute x30, waiting for transfers between devices, permute(): return lax.ppermute(block, ('replica', 'tensor'), route)  160 us
    pallas_call x9, Pallas kernels, run(): out = kernel(turn[0], *args)  51.6 us
    ppermute x30, starting transfers between devices, permute(): return lax.ppermute(block, ('replica', 'tensor'), route)  44.6 us
  transfers between devices with their start and end apart: 30, of which 21 were waited for; matrix products, arithmetic and copies ran while one was open for 4% of the time, Pallas kernels for 10%

profile of v3, /device:TPU:1, one launch (start us, length us, event | category | flops | bytes accessed | tf_op | source)
XLA Modules:
  0.0 270.0 jit_solution(2020067638715637374)
XLA Ops:
  0.1 8.3 %forward.1 = (bf16[256,2048]{1,0:T(8,128)(2,1)S(1)}, f32[256,2048]{1,0:T(8,128)S(1)}) custom-call(s32[4]{0:T(128)S(1)} %pad_add_fusion.p.c, s32[4]{0:T(128)S(1)} %pad_add_fusion.p.c, bf16[1,2,512,1792]{3,2,1,0:T(8,128)(2,1)} %h.7, bf16[1,1792,2048]{2,1,0:T(8,128)(2,1)} %refs_19_.1, bf16[1,1792,2048]{2,1,0:T(8,128)(2,1)} %refs_19_.1), custom_call_target="tpu_custom_call" | custom-call | flops 1 | bytes 1 | tf_op jit(solution)/shard_map/forward/pallas_call | solution.py:74
  23.1 11.9 %collective-permute-done.1.ha = bf16[512,768]{1,0:T(8,128)(2,1)S(1)} collective-permute-done((bf16[512,768]{1,0:T(8,128)(2,1)}, bf16[512,768]{1,0:T(8,128)(2,1)S(1)}, u32[]{:S(2)}, u32[]{:S(2)}) %collective-permute-start.1) | collective-permute-done | bytes 786464 | tf_op jit(solution)/shard_map/ppermute | solution.py:71
  37.5 2.8 %norm_backward.2.refs_0_ = bf16[256,2048]{1,0:T(8,128)(2,1)S(1)} custom-call(s32[4]{0:T(128)S(1)} %pad_add_fusion.p.c, s32[4]{0:T(128)S(1)} %pad_add_fusion.p.c, bf16[256,2048]{1,0:T(8,128)(2,1)S(1)} %add_convert_fusion.7.s, bf16[256,2048]{1,0:T(8,128)(2,1)S(1)} %collective-permute-done.2.r, bf16[1,2,512,2048]{3,2,1,0:T(8,128)(2,1)} %t.3, f32[1,2048]{1,0:T(1,128)S(1)} %bitcast.12), custom_call_target="tpu_custom_call" | custom-call | flops 1 | bytes 1 | tf_op jit(solution)/shard_map/norm_backward/pallas_call | solution.py:74
  43.5 2.9 %update.2 = bf16[256,2048]{1,0:T(8,128)(2,1)S(1)} custom-call(s32[4]{0:T(128)S(1)} %pad_add_fusion.p.c, s32[4]{0:T(128)S(1)} %pad_add_fusion.p.c, bf16[256,2048]{1,0:T(8,128)(2,1)S(1)} %norm_backward.2.refs_0_, bf16[256,2048]{1,0:T(8,128)(2,1)S(1)} %collective-permute-done.3.refs_1_, bf16[1,2,512,1792]{3,2,1,0:T(8,128)(2,1)} %h.7, ...), custom_call_target="tpu_custom_call" | custom-call | flops 1 | bytes 1 | tf_op jit(solution)/shard_map/update/pallas_call | solution.py:74
  46.5 3.5 %collective-permute-start.4 = (bf16[256,2048]{1,0:T(8,128)(2,1)S(1)}, bf16[256,2048]{1,0:T(8,128)(2,1)}, u32[]{:S(2)}, u32[]{:S(2)}) collective-permute-start(bf16[256,2048]{1,0:T(8,128)(2,1)S(1)} %update.2), channel_id=1, source_target_pairs={{0,4},{1,5},{2,6},{3,7},{4,0},{5,1},{6,2},{7,3},{8,12},{9,13},{10,... | collective-permute-start | bytes 3145736 | tf_op jit(solution)/shard_map/ppermute | solution.py:71
  51.2 7.9 %update.3 = (bf16[256,2048]{1,0:T(8,128)(2,1)S(1)}, bf16[256,2048]{1,0:T(8,128)(2,1)S(1)}, bf16[256,2048]{1,0:T(8,128)(2,1)S(1)}, bf16[256,2048]{1,0:T(8,128)(2,...) custom-call(s32[4]{0:T(128)S(1)} %pad_add_fusion.p.c, s32[4]{0:T(128)S(1)} %pad_add_fusion.p.c, ...), custom_call_target="tpu_custom_call" | custom-call | flops 1 | bytes 1 | tf_op jit(solution)/shard_map/update/pallas_call | solution.py:74
  59.3 14.0 %collective-permute-done.4 = bf16[256,2048]{1,0:T(8,128)(2,1)} collective-permute-done((bf16[256,2048]{1,0:T(8,128)(2,1)S(1)}, bf16[256,2048]{1,0:T(8,128)(2,1)}, u32[]{:S(2)}, u32[]{:S(2)}) %collective-permute-start.4) | collective-permute-done | bytes 1048608 | tf_op jit(solution)/shard_map/ppermute | solution.py:71
  78.9 16.8 %collective-permute-done.6 = bf16[256,2048]{1,0:T(8,128)(2,1)S(1)} collective-permute-done((bf16[256,2048]{1,0:T(8,128)(2,1)S(1)}, bf16[256,2048]{1,0:T(8,128)(2,1)S(1)}, u32[]{:S(2)}, u32[]{:S(2)}) %collective-permute-start.6) | collective-permute-done | bytes 1048608 | tf_op jit(solution)/shard_map/ppermute | solution.py:71
  100.1 18.1 %collective-permute-done.7 = bf16[256,2048]{1,0:T(8,128)(2,1)S(1)} collective-permute-done((bf16[256,2048]{1,0:T(8,128)(2,1)S(1)}, bf16[256,2048]{1,0:T(8,128)(2,1)S(1)}, u32[]{:S(2)}, u32[]{:S(2)}) %collective-permute-start.7) | collective-permute-done | bytes 1048608 | tf_op jit(solution)/shard_map/ppermute | solution.py:71
  118.1 2.6 collective-permute-start.11
  122.5 18.1 %collective-permute-done.9 = bf16[256,2048]{1,0:T(8,128)(2,1)S(1)} collective-permute-done((bf16[256,2048]{1,0:T(8,128)(2,1)S(1)}, bf16[256,2048]{1,0:T(8,128)(2,1)S(1)}, u32[]{:S(2)}, u32[]{:S(2)}) %collective-permute-start.9) | collective-permute-done | bytes 1048608 | tf_op jit(solution)/shard_map/ppermute | solution.py:71
  142.4 2.6 collective-permute-start.13
  145.0 18.1 %collective-permute-done.11 = bf16[256,2048]{1,0:T(8,128)(2,1)S(1)} collective-permute-done((bf16[256,2048]{1,0:T(8,128)(2,1)S(1)}, bf16[256,2048]{1,0:T(8,128)(2,1)S(1)}, u32[]{:S(2)}, u32[]{:S(2)}) %collective-permute-start.11) | collective-permute-done | bytes 1048608 | tf_op jit(solution)/shard_map/ppermute | solution.py:71
  164.8 2.6 collective-permute-start.15
  168.7 16.8 %collective-permute-done.13 = bf16[256,2048]{1,0:T(8,128)(2,1)S(1)} collective-permute-done((bf16[256,2048]{1,0:T(8,128)(2,1)S(1)}, bf16[256,2048]{1,0:T(8,128)(2,1)S(1)}, u32[]{:S(2)}, u32[]{:S(2)}) %collective-permute-start.13) | collective-permute-done | bytes 1048608 | tf_op jit(solution)/shard_map/ppermute | solution.py:71
  187.4 6.6 %begin.1.a = f32[512,2048]{1,0:T(8,128)S(1)} custom-call(s32[4]{0:T(128)S(1)} %pad_add_fusion.p.c, s32[4]{0:T(128)S(1)} %pad_add_fusion.p.c, bf16[1,2,512,1792]{3,2,1,0:T(8,128)(2,1)} %h.7, bf16[256,2048]{1,0:T(8,128)(2,1)S(1)} %add_convert_fusion.6.refs_0_, bf16[256,2048]{1,0:T(8,128)(2,1)S(1)} %add_convert_fusion.5.refs_1_, ...), custom_call_target="tpu_custom_call" | custom-call | flops 1 | bytes 1 | tf_op jit(solution)/shard_map/begin/pallas_call | solution.py:74
  194.0 14.0 %collective-permute-done.15 = bf16[256,2048]{1,0:T(8,128)(2,1)S(1)} collective-permute-done((bf16[256,2048]{1,0:T(8,128)(2,1)S(1)}, bf16[256,2048]{1,0:T(8,128)(2,1)S(1)}, u32[]{:S(2)}, u32[]{:S(2)}) %collective-permute-start.15) | collective-permute-done | bytes 1048608 | tf_op jit(solution)/shard_map/ppermute | solution.py:71
  208.5 3.5 %finish.1 = (bf16[128,2048]{1,0:T(8,128)(2,1)S(1)}, bf16[128,2048]{1,0:T(8,128)(2,1)S(1)}, f32[128,2048]{1,0:T(8,128)S(1)}, f32[128,2048]{1,0:T(8,128)S(1)}) custom-call(s32[4]{0:T(128)S(1)} %pad_add_fusion.p.c, s32[4]{0:T(128)S(1)} %pad_add_fusion.p.c, f32[512,2048]{1,0:T(8,128)S(1)} %begin.1.a, bf16[1,2,512,1792]{3,2,1,0:T(8,128)(2,1)} %h.7, ...), custom_call_target="tpu_custom_call" | custom-call | flops 1 | bytes 1 | tf_op jit(solution)/shard_map/finish/pallas_call | solution.py:74
  215.8 10.5 %collective-permute-done.21.xt = bf16[128,2048]{1,0:T(8,128)(2,1)S(1)} collective-permute-done((bf16[128,2048]{1,0:T(8,128)(2,1)S(1)}, bf16[128,2048]{1,0:T(8,128)(2,1)S(1)}, u32[]{:S(2)}, u32[]{:S(2)}) %collective-permute-start.21) | collective-permute-done | bytes 524320 | tf_op jit(solution)/shard_map/ppermute | solution.py:71
  234.1 7.0 %collective-permute-done.23.q0 = bf16[128,2048]{1,0:T(8,128)(2,1)S(1)} collective-permute-done((bf16[128,2048]{1,0:T(8,128)(2,1)S(1)}, bf16[128,2048]{1,0:T(8,128)(2,1)S(1)}, u32[]{:S(2)}, u32[]{:S(2)}) %collective-permute-start.23) | collective-permute-done | bytes 524320 | tf_op jit(solution)/shard_map/ppermute | solution.py:71
  242.0 3.0 %collective-permute-start.25 = (bf16[128,2048]{1,0:T(8,128)(2,1)S(1)}, bf16[128,2048]{1,0:T(8,128)(2,1)S(1)}, u32[]{:S(2)}, u32[]{:S(2)}) collective-permute-start(bf16[128,2048]{1,0:T(8,128)(2,1)S(1)} %collective-permute-done.22.q1), channel_id=1, source_target_pairs={{0,1},{1,0},{2,3},{3,2},{4,5},{5,4},{6,7},{7,6},{8,9},{9,8},{10,11... | collective-permute-start | bytes 1572872 | tf_op jit(solution)/shard_map/ppermute | solution.py:71
  247.2 8.4 %output_own.1.b = bf16[1,1792,2048]{2,1,0:T(8,128)(2,1)S(1)} custom-call(s32[4]{0:T(128)S(1)} %pad_add_fusion.p.c, f32[2]{0:T(128)S(1)} %pad_maximum_fusion.c, bf16[1,2,512,1792]{3,2,1,0:T(8,128)(2,1)} %h.7, bf16[128,2048]{1,0:T(8,128)(2,1)S(1)} %norm_backward.3.q0, bf16[128,2048]{1,0:T(8,128)(2,1)S(1)} %collective-permute-done.22.q1, ...), custom_call_target="tpu_custom_call" | custom-call | flops 1 | bytes 1 | tf_op jit(solution)/shard_map/output_own/pallas_call | solution.py:74
  255.6 3.0 %collective-permute-done.26.q1 = bf16[128,2048]{1,0:T(8,128)(2,1)S(1)} collective-permute-done((bf16[128,2048]{1,0:T(8,128)(2,1)S(1)}, bf16[128,2048]{1,0:T(8,128)(2,1)S(1)}, u32[]{:S(2)}, u32[]{:S(2)}) %collective-permute-start.26) | collective-permute-done | bytes 524320 | tf_op jit(solution)/shard_map/ppermute | solution.py:71
  260.9 9.1 %output_far.1 = bf16[1,1792,2048]{2,1,0:T(8,128)(2,1)} custom-call(s32[4]{0:T(128)S(1)} %pad_add_fusion.p.c, f32[2]{0:T(128)S(1)} %pad_maximum_fusion.c, bf16[512,768]{1,0:T(8,128)(2,1)S(1)} %copy-done.1, bf16[512,1024]{1,0:T(8,128)(2,1)} %collective-permute-done.5.hb, bf16[128,2048]{1,0:T(8,128)(2,1)S(1)} %collective-permute-done.23.q0, ...), custom_call_target="tpu_custom_call" | custom-call | flops 1 | bytes 1 | tf_op jit(solution)/shard_map/output_far/pallas_call | solution.py:74
  (70 shorter events, 55.1 us)
Async XLA Ops:
  12.5 25.0 %collective-permute-start.2 = (bf16[256,2048]{1,0:T(8,128)(2,1)S(1)}, bf16[256,2048]{1,0:T(8,128)(2,1)S(1)}, u32[]{:S(2)}, u32[]{:S(2)}) collective-permute-start(bf16[256,2048]{1,0:T(8,128)(2,1)S(1)} %add_convert_fusion.7.s), channel_id=1, source_target_pairs={{0,2},{1,3},{2,0},{3,1},{4,6},{5,7},{6,4},{7,5},{8,10},{9,11},{10,... | collective-permute-start | bytes 3145736 | tf_op jit(solution)/shard_map/ppermute | solution.py:71
  16.3 18.6 %collective-permute-start.1 = (bf16[512,768]{1,0:T(8,128)(2,1)}, bf16[512,768]{1,0:T(8,128)(2,1)S(1)}, u32[]{:S(2)}, u32[]{:S(2)}) collective-permute-start(bf16[512,768]{1,0:T(8,128)(2,1)} %slice_bitcast_fusion.1), channel_id=1, source_target_pairs={{0,8},{1,9},{2,10},{3,11},{4,12},{5,13},{6,14},{7,15},{8,0},{9,1},... | collective-permute-start | bytes 2359304 | tf_op jit(solution)/shard_map/ppermute | solution.py:71
  46.5 26.8 %collective-permute-start.4 = (bf16[256,2048]{1,0:T(8,128)(2,1)S(1)}, bf16[256,2048]{1,0:T(8,128)(2,1)}, u32[]{:S(2)}, u32[]{:S(2)}) collective-permute-start(bf16[256,2048]{1,0:T(8,128)(2,1)S(1)} %update.2), channel_id=1, source_target_pairs={{0,4},{1,5},{2,6},{3,7},{4,0},{5,1},{6,2},{7,3},{8,12},{9,13},{10,... | collective-permute-start | bytes 3145736 | tf_op jit(solution)/shard_map/ppermute | solution.py:71
  50.0 24.4 %collective-permute-start.5 = (bf16[512,1024]{1,0:T(8,128)(2,1)}, bf16[512,1024]{1,0:T(8,128)(2,1)}, u32[]{:S(2)}, u32[]{:S(2)}) collective-permute-start(bf16[512,1024]{1,0:T(8,128)(2,1)} %slice_bitcast_fusion), channel_id=1, source_target_pairs={{0,8},{1,9},{2,10},{3,11},{4,12},{5,13},{6,14},{7,15},{8,0},{9,1},... | collective-permute-start | bytes 3145736 | tf_op jit(solution)/shard_map/ppermute | solution.py:71
  59.1 36.6 %collective-permute-start.6 = (bf16[256,2048]{1,0:T(8,128)(2,1)S(1)}, bf16[256,2048]{1,0:T(8,128)(2,1)S(1)}, u32[]{:S(2)}, u32[]{:S(2)}) collective-permute-start(bf16[256,2048]{1,0:T(8,128)(2,1)S(1)} %get-tuple-element.112), channel_id=1, source_target_pairs={{0,4},{1,5},{2,6},{3,7},{4,0},{5,1},{6,2},{7,3},{8,12},{9,13},{10,... | collective-permute-start | bytes 3145736 | tf_op jit(solution)/shard_map/ppermute | solution.py:71
  74.3 43.8 %collective-permute-start.7 = (bf16[256,2048]{1,0:T(8,128)(2,1)S(1)}, bf16[256,2048]{1,0:T(8,128)(2,1)S(1)}, u32[]{:S(2)}, u32[]{:S(2)}) collective-permute-start(bf16[256,2048]{1,0:T(8,128)(2,1)S(1)} %get-tuple-element.115), channel_id=1, source_target_pairs={{0,4},{1,5},{2,6},{3,7},{4,0},{5,1},{6,2},{7,3},{8,12},{9,13},{10,... | collective-permute-start | bytes 3145736 | tf_op jit(solution)/shard_map/ppermute | solution.py:71
  77.6 40.6 %collective-permute-start.8 = (bf16[256,2048]{1,0:T(8,128)(2,1)S(1)}, bf16[256,2048]{1,0:T(8,128)(2,1)S(1)}, u32[]{:S(2)}, u32[]{:S(2)}) collective-permute-start(bf16[256,2048]{1,0:T(8,128)(2,1)S(1)} %add_convert_fusion.6.refs_0_), channel_id=1, source_target_pairs={{0,8},{1,9},{2,10},{3,11},{4,12},{5,13},{6,14},{7,15},{8,0},{9,1},... | collective-permute-start | bytes 3145736 | tf_op jit(solution)/shard_map/ppermute | solution.py:71
  95.7 44.9 %collective-permute-start.9 = (bf16[256,2048]{1,0:T(8,128)(2,1)S(1)}, bf16[256,2048]{1,0:T(8,128)(2,1)S(1)}, u32[]{:S(2)}, u32[]{:S(2)}) collective-permute-start(bf16[256,2048]{1,0:T(8,128)(2,1)S(1)} %get-tuple-element.119), channel_id=1, source_target_pairs={{0,4},{1,5},{2,6},{3,7},{4,0},{5,1},{6,2},{7,3},{8,12},{9,13},{10,... | collective-permute-start | bytes 3145736 | tf_op jit(solution)/shard_map/ppermute | solution.py:71
  98.8 41.8 %collective-permute-start.10 = (bf16[256,2048]{1,0:T(8,128)(2,1)S(1)}, bf16[256,2048]{1,0:T(8,128)(2,1)S(1)}, u32[]{:S(2)}, u32[]{:S(2)}) collective-permute-start(bf16[256,2048]{1,0:T(8,128)(2,1)S(1)} %add_convert_fusion.5.refs_1_), channel_id=1, source_target_pairs={{0,8},{1,9},{2,10},{3,11},{4,12},{5,13},{6,14},{7,15},{8,0},{9,1},... | collective-permute-start | bytes 3145736 | tf_op jit(solution)/shard_map/ppermute | solution.py:71
  118.1 44.9 %collective-permute-start.11 = (bf16[256,2048]{1,0:T(8,128)(2,1)S(1)}, bf16[256,2048]{1,0:T(8,128)(2,1)S(1)}, u32[]{:S(2)}, u32[]{:S(2)}) collective-permute-start(bf16[256,2048]{1,0:T(8,128)(2,1)S(1)} %get-tuple-element.123), channel_id=1, source_target_pairs={{0,4},{1,5},{2,6},{3,7},{4,0},{5,1},{6,2},{7,3},{8,12},{9,13},{10,... | collective-permute-start | bytes 3145736 | tf_op jit(solution)/shard_map/ppermute | solution.py:71
  121.2 41.8 %collective-permute-start.12 = (bf16[256,2048]{1,0:T(8,128)(2,1)S(1)}, bf16[256,2048]{1,0:T(8,128)(2,1)S(1)}, u32[]{:S(2)}, u32[]{:S(2)}) collective-permute-start(bf16[256,2048]{1,0:T(8,128)(2,1)S(1)} %add_convert_fusion.4.refs_2_), channel_id=1, source_target_pairs={{0,8},{1,9},{2,10},{3,11},{4,12},{5,13},{6,14},{7,15},{8,0},{9,1},... | collective-permute-start | bytes 3145736 | tf_op jit(solution)/shard_map/ppermute | solution.py:71
  141.1 27.6 %collective-permute-start.14 = (bf16[256,2048]{1,0:T(8,128)(2,1)S(1)}, bf16[256,2048]{1,0:T(8,128)(2,1)S(1)}, u32[]{:S(2)}, u32[]{:S(2)}) collective-permute-start(bf16[256,2048]{1,0:T(8,128)(2,1)S(1)} %add_convert_fusion.3.refs_3_), channel_id=1, source_target_pairs={{0,8},{1,9},{2,10},{3,11},{4,12},{5,13},{6,14},{7,15},{8,0},{9,1},... | collective-permute-start | bytes 3145736 | tf_op jit(solution)/shard_map/ppermute | solution.py:71
  142.4 43.2 %collective-permute-start.13 = (bf16[256,2048]{1,0:T(8,128)(2,1)S(1)}, bf16[256,2048]{1,0:T(8,128)(2,1)S(1)}, u32[]{:S(2)}, u32[]{:S(2)}) collective-permute-start(bf16[256,2048]{1,0:T(8,128)(2,1)S(1)} %get-tuple-element.127), channel_id=1, source_target_pairs={{0,4},{1,5},{2,6},{3,7},{4,0},{5,1},{6,2},{7,3},{8,12},{9,13},{10,... | collective-permute-start | bytes 3145736 | tf_op jit(solution)/shard_map/ppermute | solution.py:71
  163.5 30.5 %collective-permute-start.16 = (bf16[256,2048]{1,0:T(8,128)(2,1)S(1)}, bf16[256,2048]{1,0:T(8,128)(2,1)S(1)}, u32[]{:S(2)}, u32[]{:S(2)}) collective-permute-start(bf16[256,2048]{1,0:T(8,128)(2,1)S(1)} %add_convert_fusion.2.refs_4_), channel_id=1, source_target_pairs={{0,8},{1,9},{2,10},{3,11},{4,12},{5,13},{6,14},{7,15},{8,0},{9,1},... | collective-permute-start | bytes 3145736 | tf_op jit(solution)/shard_map/ppermute | solution.py:71
  164.8 43.2 %collective-permute-start.15 = (bf16[256,2048]{1,0:T(8,128)(2,1)S(1)}, bf16[256,2048]{1,0:T(8,128)(2,1)S(1)}, u32[]{:S(2)}, u32[]{:S(2)}) collective-permute-start(bf16[256,2048]{1,0:T(8,128)(2,1)S(1)} %get-tuple-element.130), channel_id=1, source_target_pairs={{0,4},{1,5},{2,6},{3,7},{4,0},{5,1},{6,2},{7,3},{8,12},{9,13},{10,... | collective-permute-start | bytes 3145736 | tf_op jit(solution)/shard_map/ppermute | solution.py:71
  186.0 28.6 %collective-permute-start.19 = (bf16[256,2048]{1,0:T(8,128)(2,1)S(1)}, bf16[256,2048]{1,0:T(8,128)(2,1)S(1)}, u32[]{:S(2)}, u32[]{:S(2)}) collective-permute-start(bf16[256,2048]{1,0:T(8,128)(2,1)S(1)} %add_convert_fusion.1.refs_5_), channel_id=1, source_target_pairs={{0,8},{1,9},{2,10},{3,11},{4,12},{5,13},{6,14},{7,15},{8,0},{9,1},... | collective-permute-start | bytes 3145736 | tf_op jit(solution)/shard_map/ppermute | solution.py:71
  213.1 13.2 %collective-permute-start.21 = (bf16[128,2048]{1,0:T(8,128)(2,1)S(1)}, bf16[128,2048]{1,0:T(8,128)(2,1)S(1)}, u32[]{:S(2)}, u32[]{:S(2)}) collective-permute-start(bf16[128,2048]{1,0:T(8,128)(2,1)S(1)} %get-tuple-element.168), channel_id=1, source_target_pairs={{0,8},{1,9},{2,10},{3,11},{4,12},{5,13},{6,14},{7,15},{8,0},{9,1},... | collective-permute-start | bytes 1572872 | tf_op jit(solution)/shard_map/ppermute | solution.py:71
  214.6 12.6 %collective-permute-start.20 = (bf16[128,2048]{1,0:T(8,128)(2,1)S(1)}, bf16[128,2048]{1,0:T(8,128)(2,1)S(1)}, u32[]{:S(2)}, u32[]{:S(2)}) collective-permute-start(bf16[128,2048]{1,0:T(8,128)(2,1)S(1)} %add_convert_fusion.8), channel_id=1, source_target_pairs={{0,2},{1,3},{2,0},{3,1},{4,6},{5,7},{6,4},{7,5},{8,10},{9,11},{10,... | collective-permute-start | bytes 1572872 | tf_op jit(solution)/shard_map/ppermute | solution.py:71
  229.4 11.7 %collective-permute-start.23 = (bf16[128,2048]{1,0:T(8,128)(2,1)S(1)}, bf16[128,2048]{1,0:T(8,128)(2,1)S(1)}, u32[]{:S(2)}, u32[]{:S(2)}) collective-permute-start(bf16[128,2048]{1,0:T(8,128)(2,1)S(1)} %norm_backward.3.q0), channel_id=1, source_target_pairs={{0,8},{1,9},{2,10},{3,11},{4,12},{5,13},{6,14},{7,15},{8,0},{9,1},... | collective-permute-start | bytes 1572872 | tf_op jit(solution)/shard_map/ppermute | solution.py:71
  230.7 11.3 %collective-permute-start.22 = (bf16[128,2048]{1,0:T(8,128)(2,1)S(1)}, bf16[128,2048]{1,0:T(8,128)(2,1)S(1)}, u32[]{:S(2)}, u32[]{:S(2)}) collective-permute-start(bf16[128,2048]{1,0:T(8,128)(2,1)S(1)} %norm_backward.3.q0), channel_id=1, source_target_pairs={{0,2},{1,3},{2,0},{3,1},{4,6},{5,7},{6,4},{7,5},{8,10},{9,11},{10,... | collective-permute-start | bytes 1572872 | tf_op jit(solution)/shard_map/ppermute | solution.py:71
  232.0 15.1 %collective-permute-start.24 = (bf16[128,2048]{1,0:T(8,128)(2,1)S(1)}, bf16[128,2048]{1,0:T(8,128)(2,1)S(1)}, u32[]{:S(2)}, u32[]{:S(2)}) collective-permute-start(bf16[128,2048]{1,0:T(8,128)(2,1)S(1)} %norm_backward.3.q0), channel_id=1, source_target_pairs={{0,1},{1,0},{2,3},{3,2},{4,5},{5,4},{6,7},{7,6},{8,9},{9,8},{10,11... | collective-permute-start | bytes 1572872 | tf_op jit(solution)/shard_map/ppermute | solution.py:71
  245.0 13.6 %collective-permute-start.26 = (bf16[128,2048]{1,0:T(8,128)(2,1)S(1)}, bf16[128,2048]{1,0:T(8,128)(2,1)S(1)}, u32[]{:S(2)}, u32[]{:S(2)}) collective-permute-start(bf16[128,2048]{1,0:T(8,128)(2,1)S(1)} %collective-permute-done.23.q0), channel_id=1, source_target_pairs={{0,2},{1,3},{2,0},{3,1},{4,6},{5,7},{6,4},{7,5},{8,10},{9,11},{10,... | collective-permute-start | bytes 1572872 | tf_op jit(solution)/shard_map/ppermute | solution.py:71
  246.3 13.2 %collective-permute-start.29 = (bf16[128,2048]{1,0:T(8,128)(2,1)S(1)}, bf16[128,2048]{1,0:T(8,128)(2,1)S(1)}, u32[]{:S(2)}, u32[]{:S(2)}) collective-permute-start(bf16[128,2048]{1,0:T(8,128)(2,1)S(1)} %get-tuple-element.165), channel_id=1, source_target_pairs={{0,8},{1,9},{2,10},{3,11},{4,12},{5,13},{6,14},{7,15},{8,0},{9,1},... | collective-permute-start | bytes 1572872 | tf_op jit(solution)/shard_map/ppermute | solution.py:71
  246.6 13.0 %collective-permute-start.27 = (bf16[128,2048]{1,0:T(8,128)(2,1)S(1)}, bf16[128,2048]{1,0:T(8,128)(2,1)S(1)}, u32[]{:S(2)}, u32[]{:S(2)}) collective-permute-start(bf16[128,2048]{1,0:T(8,128)(2,1)S(1)} %collective-permute-done.23.q0), channel_id=1, source_target_pairs={{0,1},{1,0},{2,3},{3,2},{4,5},{5,4},{6,7},{7,6},{8,9},{9,8},{10,11... | collective-permute-start | bytes 1572872 | tf_op jit(solution)/shard_map/ppermute | solution.py:71
  (10 other events, 86.4 us)

commit v4 on v3

--- a/solution.py
+++ b/solution.py
@@ -225,17 +225,17 @@
         return run(
             call(
                 body,
-                (4,),
+                (2,),
                 [
-                    grid_block((tokens, cols)),
+                    grid_block((tokens, 2 * cols)),
                     pl.BlockSpec((1, 1, tokens, 2 * unit), lambda n, p, c: (0, 1, 0, UNITS // 2 - 1)),
-                    grid_block((2 * unit, cols)),
+                    grid_block((2 * unit, 2 * cols)),
                 ],
-                [grid_block((quarter, cols))] * 4,
+                [grid_block((quarter, 2 * cols))] * 4,
                 [jax.ShapeDtypeStruct((quarter, features), kind) for kind in kinds],
                 "finish",
-                10,
-                scratch=[pltpu.VMEM((tokens, cols), jnp.float32)],
+                20,
+                scratch=[pltpu.VMEM((tokens, 2 * cols), jnp.float32)],
             ),
             place,
             begun,
@@ -386,16 +386,15 @@
 
     sent_out, sent_stay, kept_out, kept_stay = finish(begun, averaged[-1])
     outgoing = add(kept_out, permute(sent_out, 0, 1))
-    outgoing, x_got[-1] = meet(outgoing, x_got[-1])
+    outgoing, top, x_got[-1] = meet(outgoing, averaged[-1][:unit], x_got[-1])
     incoming = permute(outgoing, 0, 2)
-    x_top = permute(averaged[-1][:unit], 2, 0)
-    incoming, x_top = meet(incoming, x_top)
+    x_top = permute(top, 2, 0)
     staying = kept_stay + permute(sent_stay, 0, 1).astype(jnp.float32)
     mine_q = norm_backward(1, staying, incoming)
     final, mine_q = meet(averaged[-1][unit:], mine_q)
     near_q = permute(mine_q, 0, 2)
     far_q = permute(mine_q, 2, 0)
-    near_q, far_q = meet(near_q, far_q)
+    near_q, far_q, x_top = meet(near_q, far_q, x_top)
     far_near = permute(far_q, 0, 2)
     x_low = permute(final, 2, 0)
     base = output_own((mine_q, near_q, permute(mine_q, 0, 1), permute(near_q, 0, 1)), averaged, x_got)

time: 271 us -> 270 us (level)
  transfers between devices with their start and end apart: 30 -> 30, of which waited for: 21 -> 20; matrix products, arithmetic and copies ran while one was open for 4% -> 4% of each run, Pallas kernels for 10% -> 10%
where the time goes in v4:
time: 270 us; the launch traced here: 269 us
  waiting for transfers between devices  159 us (59%)
  Pallas kernels  51.3 us (19%)
  starting transfers between devices  45.3 us (17%)
  local copies, waits for them, and re-layouts  5.99 us (2%)
  other arithmetic  4.93 us (2%)
  between operations  2.77 us (1%)
    ppermute x30, waiting for transfers between devices, permute(): return lax.ppermute(block, ('replica', 'tensor'), route)  159 us
    pallas_call x9, Pallas kernels, run(): out = kernel(turn[0], *args)  51.3 us
    ppermute x30, starting transfers between devices, permute(): return lax.ppermute(block, ('replica', 'tensor'), route)  45.3 us
  transfers between devices with their start and end apart: 30, of which 20 were waited for; matrix products, arithmetic and copies ran while one was open for 4% of the time, Pallas kernels for 10%

profile of v4, /device:TPU:1, one launch (start us, length us, event | category | flops | bytes accessed | tf_op | source)
XLA Modules:
  0.0 269.2 jit_solution(6078690393947470392)
XLA Ops:
  0.1 8.3 %forward.1 = (bf16[256,2048]{1,0:T(8,128)(2,1)S(1)}, f32[256,2048]{1,0:T(8,128)S(1)}) custom-call(s32[4]{0:T(128)S(1)} %pad_add_fusion.p.c, s32[4]{0:T(128)S(1)} %pad_add_fusion.p.c, bf16[1,2,512,1792]{3,2,1,0:T(8,128)(2,1)} %h.7, bf16[1,1792,2048]{2,1,0:T(8,128)(2,1)} %refs_19_.1, bf16[1,1792,2048]{2,1,0:T(8,128)(2,1)} %refs_19_.1), custom_call_target="tpu_custom_call" | custom-call | flops 1 | bytes 1 | tf_op jit(solution)/shard_map/forward/pallas_call | solution.py:74
  23.1 11.9 %collective-permute-done.1.ha = bf16[512,768]{1,0:T(8,128)(2,1)S(1)} collective-permute-done((bf16[512,768]{1,0:T(8,128)(2,1)}, bf16[512,768]{1,0:T(8,128)(2,1)S(1)}, u32[]{:S(2)}, u32[]{:S(2)}) %collective-permute-start.1) | collective-permute-done | bytes 786464 | tf_op jit(solution)/shard_map/ppermute | solution.py:71
  37.5 2.8 %norm_backward.2.refs_0_ = bf16[256,2048]{1,0:T(8,128)(2,1)S(1)} custom-call(s32[4]{0:T(128)S(1)} %pad_add_fusion.p.c, s32[4]{0:T(128)S(1)} %pad_add_fusion.p.c, bf16[256,2048]{1,0:T(8,128)(2,1)S(1)} %add_convert_fusion.7.s, bf16[256,2048]{1,0:T(8,128)(2,1)S(1)} %collective-permute-done.2.r, bf16[1,2,512,2048]{3,2,1,0:T(8,128)(2,1)} %t.3, f32[1,2048]{1,0:T(1,128)S(1)} %bitcast.12), custom_call_target="tpu_custom_call" | custom-call | flops 1 | bytes 1 | tf_op jit(solution)/shard_map/norm_backward/pallas_call | solution.py:74
  43.5 2.9 %update.2 = bf16[256,2048]{1,0:T(8,128)(2,1)S(1)} custom-call(s32[4]{0:T(128)S(1)} %pad_add_fusion.p.c, s32[4]{0:T(128)S(1)} %pad_add_fusion.p.c, bf16[256,2048]{1,0:T(8,128)(2,1)S(1)} %norm_backward.2.refs_0_, bf16[256,2048]{1,0:T(8,128)(2,1)S(1)} %collective-permute-done.3.refs_1_, bf16[1,2,512,1792]{3,2,1,0:T(8,128)(2,1)} %h.7, ...), custom_call_target="tpu_custom_call" | custom-call | flops 1 | bytes 1 | tf_op jit(solution)/shard_map/update/pallas_call | solution.py:74
  46.5 3.5 %collective-permute-start.4 = (bf16[256,2048]{1,0:T(8,128)(2,1)S(1)}, bf16[256,2048]{1,0:T(8,128)(2,1)}, u32[]{:S(2)}, u32[]{:S(2)}) collective-permute-start(bf16[256,2048]{1,0:T(8,128)(2,1)S(1)} %update.2), channel_id=1, source_target_pairs={{0,4},{1,5},{2,6},{3,7},{4,0},{5,1},{6,2},{7,3},{8,12},{9,13},{10,... | collective-permute-start | bytes 3145736 | tf_op jit(solution)/shard_map/ppermute | solution.py:71
  51.2 7.9 %update.3 = (bf16[256,2048]{1,0:T(8,128)(2,1)S(1)}, bf16[256,2048]{1,0:T(8,128)(2,1)S(1)}, bf16[256,2048]{1,0:T(8,128)(2,1)S(1)}, bf16[256,2048]{1,0:T(8,128)(2,...) custom-call(s32[4]{0:T(128)S(1)} %pad_add_fusion.p.c, s32[4]{0:T(128)S(1)} %pad_add_fusion.p.c, ...), custom_call_target="tpu_custom_call" | custom-call | flops 1 | bytes 1 | tf_op jit(solution)/shard_map/update/pallas_call | solution.py:74
  59.3 14.0 %collective-permute-done.4 = bf16[256,2048]{1,0:T(8,128)(2,1)} collective-permute-done((bf16[256,2048]{1,0:T(8,128)(2,1)S(1)}, bf16[256,2048]{1,0:T(8,128)(2,1)}, u32[]{:S(2)}, u32[]{:S(2)}) %collective-permute-start.4) | collective-permute-done | bytes 1048608 | tf_op jit(solution)/shard_map/ppermute | solution.py:71
  78.9 16.8 %collective-permute-done.6 = bf16[256,2048]{1,0:T(8,128)(2,1)S(1)} collective-permute-done((bf16[256,2048]{1,0:T(8,128)(2,1)S(1)}, bf16[256,2048]{1,0:T(8,128)(2,1)S(1)}, u32[]{:S(2)}, u32[]{:S(2)}) %collective-permute-start.6) | collective-permute-done | bytes 1048608 | tf_op jit(solution)/shard_map/ppermute | solution.py:71
  100.1 18.1 %collective-permute-done.7 = bf16[256,2048]{1,0:T(8,128)(2,1)S(1)} collective-permute-done((bf16[256,2048]{1,0:T(8,128)(2,1)S(1)}, bf16[256,2048]{1,0:T(8,128)(2,1)S(1)}, u32[]{:S(2)}, u32[]{:S(2)}) %collective-permute-start.7) | collective-permute-done | bytes 1048608 | tf_op jit(solution)/shard_map/ppermute | solution.py:71
  118.1 2.6 collective-permute-start.11
  122.5 18.1 %collective-permute-done.9 = bf16[256,2048]{1,0:T(8,128)(2,1)S(1)} collective-permute-done((bf16[256,2048]{1,0:T(8,128)(2,1)S(1)}, bf16[256,2048]{1,0:T(8,128)(2,1)S(1)}, u32[]{:S(2)}, u32[]{:S(2)}) %collective-permute-start.9) | collective-permute-done | bytes 1048608 | tf_op jit(solution)/shard_map/ppermute | solution.py:71
  142.4 2.6 collective-permute-start.13
  145.0 18.1 %collective-permute-done.11 = bf16[256,2048]{1,0:T(8,128)(2,1)S(1)} collective-permute-done((bf16[256,2048]{1,0:T(8,128)(2,1)S(1)}, bf16[256,2048]{1,0:T(8,128)(2,1)S(1)}, u32[]{:S(2)}, u32[]{:S(2)}) %collective-permute-start.11) | collective-permute-done | bytes 1048608 | tf_op jit(solution)/shard_map/ppermute | solution.py:71
  164.8 2.6 collective-permute-start.15
  168.7 16.8 %collective-permute-done.13 = bf16[256,2048]{1,0:T(8,128)(2,1)S(1)} collective-permute-done((bf16[256,2048]{1,0:T(8,128)(2,1)S(1)}, bf16[256,2048]{1,0:T(8,128)(2,1)S(1)}, u32[]{:S(2)}, u32[]{:S(2)}) %collective-permute-start.13) | collective-permute-done | bytes 1048608 | tf_op jit(solution)/shard_map/ppermute | solution.py:71
  187.4 6.6 %begin.1.a = f32[512,2048]{1,0:T(8,128)S(1)} custom-call(s32[4]{0:T(128)S(1)} %pad_add_fusion.p.c, s32[4]{0:T(128)S(1)} %pad_add_fusion.p.c, bf16[1,2,512,1792]{3,2,1,0:T(8,128)(2,1)} %h.7, bf16[256,2048]{1,0:T(8,128)(2,1)S(1)} %add_convert_fusion.6.refs_0_, bf16[256,2048]{1,0:T(8,128)(2,1)S(1)} %add_convert_fusion.5.refs_1_, ...), custom_call_target="tpu_custom_call" | custom-call | flops 1 | bytes 1 | tf_op jit(solution)/shard_map/begin/pallas_call | solution.py:74
  194.0 14.0 %collective-permute-done.15 = bf16[256,2048]{1,0:T(8,128)(2,1)S(1)} collective-permute-done((bf16[256,2048]{1,0:T(8,128)(2,1)S(1)}, bf16[256,2048]{1,0:T(8,128)(2,1)S(1)}, u32[]{:S(2)}, u32[]{:S(2)}) %collective-permute-start.15) | collective-permute-done | bytes 1048608 | tf_op jit(solution)/shard_map/ppermute | solution.py:71
  208.5 3.1 %finish.1 = (bf16[128,2048]{1,0:T(8,128)(2,1)S(1)}, bf16[128,2048]{1,0:T(8,128)(2,1)S(1)}, f32[128,2048]{1,0:T(8,128)S(1)}, f32[128,2048]{1,0:T(8,128)S(1)}) custom-call(s32[4]{0:T(128)S(1)} %pad_add_fusion.p.c, s32[4]{0:T(128)S(1)} %pad_add_fusion.p.c, f32[512,2048]{1,0:T(8,128)S(1)} %begin.1.a, bf16[1,2,512,1792]{3,2,1,0:T(8,128)(2,1)} %h.7, ...), custom_call_target="tpu_custom_call" | custom-call | flops 1 | bytes 1 | tf_op jit(solution)/shard_map/finish/pallas_call | solution.py:74
  216.6 9.8 %collective-permute-done.20.r = bf16[128,2048]{1,0:T(8,128)(2,1)S(1)} collective-permute-done((bf16[128,2048]{1,0:T(8,128)(2,1)S(1)}, bf16[128,2048]{1,0:T(8,128)(2,1)S(1)}, u32[]{:S(2)}, u32[]{:S(2)}) %collective-permute-start.20) | collective-permute-done | bytes 524320 | tf_op jit(solution)/shard_map/ppermute | solution.py:71
  233.7 6.1 %collective-permute-done.22.q0 = bf16[128,2048]{1,0:T(8,128)(2,1)S(1)} collective-permute-done((bf16[128,2048]{1,0:T(8,128)(2,1)S(1)}, bf16[128,2048]{1,0:T(8,128)(2,1)S(1)}, u32[]{:S(2)}, u32[]{:S(2)}) %collective-permute-start.22) | collective-permute-done | bytes 524320 | tf_op jit(solution)/shard_map/ppermute | solution.py:71
  240.7 3.5 %collective-permute-start.25 = (bf16[128,2048]{1,0:T(8,128)(2,1)S(1)}, bf16[128,2048]{1,0:T(8,128)(2,1)S(1)}, u32[]{:S(2)}, u32[]{:S(2)}) collective-permute-start(bf16[128,2048]{1,0:T(8,128)(2,1)S(1)} %collective-permute-done.21.q1), channel_id=1, source_target_pairs={{0,1},{1,0},{2,3},{3,2},{4,5},{5,4},{6,7},{7,6},{8,9},{9,8},{10,11... | collective-permute-start | bytes 1572872 | tf_op jit(solution)/shard_map/ppermute | solution.py:71
  246.3 8.4 %output_own.1.b = bf16[1,1792,2048]{2,1,0:T(8,128)(2,1)S(1)} custom-call(s32[4]{0:T(128)S(1)} %pad_add_fusion.p.c, f32[2]{0:T(128)S(1)} %pad_maximum_fusion.c, bf16[1,2,512,1792]{3,2,1,0:T(8,128)(2,1)} %h.7, bf16[128,2048]{1,0:T(8,128)(2,1)S(1)} %norm_backward.3.q0, bf16[128,2048]{1,0:T(8,128)(2,1)S(1)} %collective-permute-done.21.q1, ...), custom_call_target="tpu_custom_call" | custom-call | flops 1 | bytes 1 | tf_op jit(solution)/shard_map/output_own/pallas_call | solution.py:74
  254.7 3.0 %collective-permute-done.26.q1 = bf16[128,2048]{1,0:T(8,128)(2,1)S(1)} collective-permute-done((bf16[128,2048]{1,0:T(8,128)(2,1)S(1)}, bf16[128,2048]{1,0:T(8,128)(2,1)S(1)}, u32[]{:S(2)}, u32[]{:S(2)}) %collective-permute-start.26) | collective-permute-done | bytes 524320 | tf_op jit(solution)/shard_map/ppermute | solution.py:71
  260.0 9.1 %output_far.1 = bf16[1,1792,2048]{2,1,0:T(8,128)(2,1)} custom-call(s32[4]{0:T(128)S(1)} %pad_add_fusion.p.c, f32[2]{0:T(128)S(1)} %pad_maximum_fusion.c, bf16[512,768]{1,0:T(8,128)(2,1)S(1)} %copy-done.1, bf16[512,1024]{1,0:T(8,128)(2,1)} %collective-permute-done.5.hb, bf16[128,2048]{1,0:T(8,128)(2,1)S(1)} %collective-permute-done.22.q0, ...), custom_call_target="tpu_custom_call" | custom-call | flops 1 | bytes 1 | tf_op jit(solution)/shard_map/output_far/pallas_call | solution.py:74
  (70 shorter events, 55.8 us)
Async XLA Ops:
  12.5 25.0 %collective-permute-start.2 = (bf16[256,2048]{1,0:T(8,128)(2,1)S(1)}, bf16[256,2048]{1,0:T(8,128)(2,1)S(1)}, u32[]{:S(2)}, u32[]{:S(2)}) collective-permute-start(bf16[256,2048]{1,0:T(8,128)(2,1)S(1)} %add_convert_fusion.7.s), channel_id=1, source_target_pairs={{0,2},{1,3},{2,0},{3,1},{4,6},{5,7},{6,4},{7,5},{8,10},{9,11},{10,... | collective-permute-start | bytes 3145736 | tf_op jit(solution)/shard_map/ppermute | solution.py:71
  16.3 18.6 %collective-permute-start.1 = (bf16[512,768]{1,0:T(8,128)(2,1)}, bf16[512,768]{1,0:T(8,128)(2,1)S(1)}, u32[]{:S(2)}, u32[]{:S(2)}) collective-permute-start(bf16[512,768]{1,0:T(8,128)(2,1)} %slice_bitcast_fusion.1), channel_id=1, source_target_pairs={{0,8},{1,9},{2,10},{3,11},{4,12},{5,13},{6,14},{7,15},{8,0},{9,1},... | collective-permute-start | bytes 2359304 | tf_op jit(solution)/shard_map/ppermute | solution.py:71
  46.5 26.8 %collective-permute-start.4 = (bf16[256,2048]{1,0:T(8,128)(2,1)S(1)}, bf16[256,2048]{1,0:T(8,128)(2,1)}, u32[]{:S(2)}, u32[]{:S(2)}) collective-permute-start(bf16[256,2048]{1,0:T(8,128)(2,1)S(1)} %update.2), channel_id=1, source_target_pairs={{0,4},{1,5},{2,6},{3,7},{4,0},{5,1},{6,2},{7,3},{8,12},{9,13},{10,... | collective-permute-start | bytes 3145736 | tf_op jit(solution)/shard_map/ppermute | solution.py:71
  50.0 24.4 %collective-permute-start.5 = (bf16[512,1024]{1,0:T(8,128)(2,1)}, bf16[512,1024]{1,0:T(8,128)(2,1)}, u32[]{:S(2)}, u32[]{:S(2)}) collective-permute-start(bf16[512,1024]{1,0:T(8,128)(2,1)} %slice_bitcast_fusion), channel_id=1, source_target_pairs={{0,8},{1,9},{2,10},{3,11},{4,12},{5,13},{6,14},{7,15},{8,0},{9,1},... | collective-permute-start | bytes 3145736 | tf_op jit(solution)/shard_map/ppermute | solution.py:71
  59.1 36.6 %collective-permute-start.6 = (bf16[256,2048]{1,0:T(8,128)(2,1)S(1)}, bf16[256,2048]{1,0:T(8,128)(2,1)S(1)}, u32[]{:S(2)}, u32[]{:S(2)}) collective-permute-start(bf16[256,2048]{1,0:T(8,128)(2,1)S(1)} %get-tuple-element.112), channel_id=1, source_target_pairs={{0,4},{1,5},{2,6},{3,7},{4,0},{5,1},{6,2},{7,3},{8,12},{9,13},{10,... | collective-permute-start | bytes 3145736 | tf_op jit(solution)/shard_map/ppermute | solution.py:71
  74.3 43.8 %collective-permute-start.7 = (bf16[256,2048]{1,0:T(8,128)(2,1)S(1)}, bf16[256,2048]{1,0:T(8,128)(2,1)S(1)}, u32[]{:S(2)}, u32[]{:S(2)}) collective-permute-start(bf16[256,2048]{1,0:T(8,128)(2,1)S(1)} %get-tuple-element.115), channel_id=1, source_target_pairs={{0,4},{1,5},{2,6},{3,7},{4,0},{5,1},{6,2},{7,3},{8,12},{9,13},{10,... | collective-permute-start | bytes 3145736 | tf_op jit(solution)/shard_map/ppermute | solution.py:71
  77.6 40.6 %collective-permute-start.8 = (bf16[256,2048]{1,0:T(8,128)(2,1)S(1)}, bf16[256,2048]{1,0:T(8,128)(2,1)S(1)}, u32[]{:S(2)}, u32[]{:S(2)}) collective-permute-start(bf16[256,2048]{1,0:T(8,128)(2,1)S(1)} %add_convert_fusion.6.refs_0_), channel_id=1, source_target_pairs={{0,8},{1,9},{2,10},{3,11},{4,12},{5,13},{6,14},{7,15},{8,0},{9,1},... | collective-permute-start | bytes 3145736 | tf_op jit(solution)/shard_map/ppermute | solution.py:71
  95.7 44.9 %collective-permute-start.9 = (bf16[256,2048]{1,0:T(8,128)(2,1)S(1)}, bf16[256,2048]{1,0:T(8,128)(2,1)S(1)}, u32[]{:S(2)}, u32[]{:S(2)}) collective-permute-start(bf16[256,2048]{1,0:T(8,128)(2,1)S(1)} %get-tuple-element.119), channel_id=1, source_target_pairs={{0,4},{1,5},{2,6},{3,7},{4,0},{5,1},{6,2},{7,3},{8,12},{9,13},{10,... | collective-permute-start | bytes 3145736 | tf_op jit(solution)/shard_map/ppermute | solution.py:71
  98.8 41.8 %collective-permute-start.10 = (bf16[256,2048]{1,0:T(8,128)(2,1)S(1)}, bf16[256,2048]{1,0:T(8,128)(2,1)S(1)}, u32[]{:S(2)}, u32[]{:S(2)}) collective-permute-start(bf16[256,2048]{1,0:T(8,128)(2,1)S(1)} %add_convert_fusion.5.refs_1_), channel_id=1, source_target_pairs={{0,8},{1,9},{2,10},{3,11},{4,12},{5,13},{6,14},{7,15},{8,0},{9,1},... | collective-permute-start | bytes 3145736 | tf_op jit(solution)/shard_map/ppermute | solution.py:71
  118.1 44.9 %collective-permute-start.11 = (bf16[256,2048]{1,0:T(8,128)(2,1)S(1)}, bf16[256,2048]{1,0:T(8,128)(2,1)S(1)}, u32[]{:S(2)}, u32[]{:S(2)}) collective-permute-start(bf16[256,2048]{1,0:T(8,128)(2,1)S(1)} %get-tuple-element.123), channel_id=1, source_target_pairs={{0,4},{1,5},{2,6},{3,7},{4,0},{5,1},{6,2},{7,3},{8,12},{9,13},{10,... | collective-permute-start | bytes 3145736 | tf_op jit(solution)/shard_map/ppermute | solution.py:71
  121.2 41.8 %collective-permute-start.12 = (bf16[256,2048]{1,0:T(8,128)(2,1)S(1)}, bf16[256,2048]{1,0:T(8,128)(2,1)S(1)}, u32[]{:S(2)}, u32[]{:S(2)}) collective-permute-start(bf16[256,2048]{1,0:T(8,128)(2,1)S(1)} %add_convert_fusion.4.refs_2_), channel_id=1, source_target_pairs={{0,8},{1,9},{2,10},{3,11},{4,12},{5,13},{6,14},{7,15},{8,0},{9,1},... | collective-permute-start | bytes 3145736 | tf_op jit(solution)/shard_map/ppermute | solution.py:71
  141.1 27.6 %collective-permute-start.14 = (bf16[256,2048]{1,0:T(8,128)(2,1)S(1)}, bf16[256,2048]{1,0:T(8,128)(2,1)S(1)}, u32[]{:S(2)}, u32[]{:S(2)}) collective-permute-start(bf16[256,2048]{1,0:T(8,128)(2,1)S(1)} %add_convert_fusion.3.refs_3_), channel_id=1, source_target_pairs={{0,8},{1,9},{2,10},{3,11},{4,12},{5,13},{6,14},{7,15},{8,0},{9,1},... | collective-permute-start | bytes 3145736 | tf_op jit(solution)/shard_map/ppermute | solution.py:71
  142.4 43.2 %collective-permute-start.13 = (bf16[256,2048]{1,0:T(8,128)(2,1)S(1)}, bf16[256,2048]{1,0:T(8,128)(2,1)S(1)}, u32[]{:S(2)}, u32[]{:S(2)}) collective-permute-start(bf16[256,2048]{1,0:T(8,128)(2,1)S(1)} %get-tuple-element.127), channel_id=1, source_target_pairs={{0,4},{1,5},{2,6},{3,7},{4,0},{5,1},{6,2},{7,3},{8,12},{9,13},{10,... | collective-permute-start | bytes 3145736 | tf_op jit(solution)/shard_map/ppermute | solution.py:71
  163.5 30.5 %collective-permute-start.16 = (bf16[256,2048]{1,0:T(8,128)(2,1)S(1)}, bf16[256,2048]{1,0:T(8,128)(2,1)S(1)}, u32[]{:S(2)}, u32[]{:S(2)}) collective-permute-start(bf16[256,2048]{1,0:T(8,128)(2,1)S(1)} %add_convert_fusion.2.refs_4_), channel_id=1, source_target_pairs={{0,8},{1,9},{2,10},{3,11},{4,12},{5,13},{6,14},{7,15},{8,0},{9,1},... | collective-permute-start | bytes 3145736 | tf_op jit(solution)/shard_map/ppermute | solution.py:71
  164.8 43.2 %collective-permute-start.15 = (bf16[256,2048]{1,0:T(8,128)(2,1)S(1)}, bf16[256,2048]{1,0:T(8,128)(2,1)S(1)}, u32[]{:S(2)}, u32[]{:S(2)}) collective-permute-start(bf16[256,2048]{1,0:T(8,128)(2,1)S(1)} %get-tuple-element.130), channel_id=1, source_target_pairs={{0,4},{1,5},{2,6},{3,7},{4,0},{5,1},{6,2},{7,3},{8,12},{9,13},{10,... | collective-permute-start | bytes 3145736 | tf_op jit(solution)/shard_map/ppermute | solution.py:71
  186.0 28.2 %collective-permute-start.19 = (bf16[256,2048]{1,0:T(8,128)(2,1)S(1)}, bf16[256,2048]{1,0:T(8,128)(2,1)S(1)}, u32[]{:S(2)}, u32[]{:S(2)}) collective-permute-start(bf16[256,2048]{1,0:T(8,128)(2,1)S(1)} %add_convert_fusion.1.refs_5_), channel_id=1, source_target_pairs={{0,8},{1,9},{2,10},{3,11},{4,12},{5,13},{6,14},{7,15},{8,0},{9,1},... | collective-permute-start | bytes 3145736 | tf_op jit(solution)/shard_map/ppermute | solution.py:71
  214.2 12.2 %collective-permute-start.20 = (bf16[128,2048]{1,0:T(8,128)(2,1)S(1)}, bf16[128,2048]{1,0:T(8,128)(2,1)S(1)}, u32[]{:S(2)}, u32[]{:S(2)}) collective-permute-start(bf16[128,2048]{1,0:T(8,128)(2,1)S(1)} %add_convert_fusion.8), channel_id=1, source_target_pairs={{0,2},{1,3},{2,0},{3,1},{4,6},{5,7},{6,4},{7,5},{8,10},{9,11},{10,... | collective-permute-start | bytes 1572872 | tf_op jit(solution)/shard_map/ppermute | solution.py:71
  215.2 18.4 %collective-permute-start.23 = (bf16[128,2048]{1,0:T(8,128)(2,1)S(1)}, bf16[128,2048]{1,0:T(8,128)(2,1)S(1)}, u32[]{:S(2)}, u32[]{:S(2)}) collective-permute-start(bf16[128,2048]{1,0:T(8,128)(2,1)S(1)} %get-tuple-element.149), channel_id=1, source_target_pairs={{0,8},{1,9},{2,10},{3,11},{4,12},{5,13},{6,14},{7,15},{8,0},{9,1},... | collective-permute-start | bytes 1572872 | tf_op jit(solution)/shard_map/ppermute | solution.py:71
  228.5 11.2 %collective-permute-start.22 = (bf16[128,2048]{1,0:T(8,128)(2,1)S(1)}, bf16[128,2048]{1,0:T(8,128)(2,1)S(1)}, u32[]{:S(2)}, u32[]{:S(2)}) collective-permute-start(bf16[128,2048]{1,0:T(8,128)(2,1)S(1)} %norm_backward.3.q0), channel_id=1, source_target_pairs={{0,8},{1,9},{2,10},{3,11},{4,12},{5,13},{6,14},{7,15},{8,0},{9,1},... | collective-permute-start | bytes 1572872 | tf_op jit(solution)/shard_map/ppermute | solution.py:71
  229.8 10.9 %collective-permute-start.21 = (bf16[128,2048]{1,0:T(8,128)(2,1)S(1)}, bf16[128,2048]{1,0:T(8,128)(2,1)S(1)}, u32[]{:S(2)}, u32[]{:S(2)}) collective-permute-start(bf16[128,2048]{1,0:T(8,128)(2,1)S(1)} %norm_backward.3.q0), channel_id=1, source_target_pairs={{0,2},{1,3},{2,0},{3,1},{4,6},{5,7},{6,4},{7,5},{8,10},{9,11},{10,... | collective-permute-start | bytes 1572872 | tf_op jit(solution)/shard_map/ppermute | solution.py:71
  231.1 15.2 %collective-permute-start.24 = (bf16[128,2048]{1,0:T(8,128)(2,1)S(1)}, bf16[128,2048]{1,0:T(8,128)(2,1)S(1)}, u32[]{:S(2)}, u32[]{:S(2)}) collective-permute-start(bf16[128,2048]{1,0:T(8,128)(2,1)S(1)} %norm_backward.3.q0), channel_id=1, source_target_pairs={{0,1},{1,0},{2,3},{3,2},{4,5},{5,4},{6,7},{7,6},{8,9},{9,8},{10,11... | collective-permute-start | bytes 1572872 | tf_op jit(solution)/shard_map/ppermute | solution.py:71
  244.2 13.6 %collective-permute-start.26 = (bf16[128,2048]{1,0:T(8,128)(2,1)S(1)}, bf16[128,2048]{1,0:T(8,128)(2,1)S(1)}, u32[]{:S(2)}, u32[]{:S(2)}) collective-permute-start(bf16[128,2048]{1,0:T(8,128)(2,1)S(1)} %collective-permute-done.22.q0), channel_id=1, source_target_pairs={{0,2},{1,3},{2,0},{3,1},{4,6},{5,7},{6,4},{7,5},{8,10},{9,11},{10,... | collective-permute-start | bytes 1572872 | tf_op jit(solution)/shard_map/ppermute | solution.py:71
  245.4 13.2 %collective-permute-start.29 = (bf16[128,2048]{1,0:T(8,128)(2,1)S(1)}, bf16[128,2048]{1,0:T(8,128)(2,1)S(1)}, u32[]{:S(2)}, u32[]{:S(2)}) collective-permute-start(bf16[128,2048]{1,0:T(8,128)(2,1)S(1)} %get-tuple-element.165), channel_id=1, source_target_pairs={{0,8},{1,9},{2,10},{3,11},{4,12},{5,13},{6,14},{7,15},{8,0},{9,1},... | collective-permute-start | bytes 1572872 | tf_op jit(solution)/shard_map/ppermute | solution.py:71
  245.7 13.0 %collective-permute-start.27 = (bf16[128,2048]{1,0:T(8,128)(2,1)S(1)}, bf16[128,2048]{1,0:T(8,128)(2,1)S(1)}, u32[]{:S(2)}, u32[]{:S(2)}) collective-permute-start(bf16[128,2048]{1,0:T(8,128)(2,1)S(1)} %collective-permute-done.22.q0), channel_id=1, source_target_pairs={{0,1},{1,0},{2,3},{3,2},{4,5},{5,4},{6,7},{7,6},{8,9},{9,8},{10,11... | collective-permute-start | bytes 1572872 | tf_op jit(solution)/shard_map/ppermute | solution.py:71
  (10 other events, 88.0 us)
